TPU v7x, 256 devices: a whole 4x4x8 slice. The times are simulated.
256 devices in a mesh: leaf: 16 (over z, core), leg: 16 (over y, x).
Axes of the slice: x: 4, y: 4, z: 8, core: 2. Of those that a mesh axis runs over, the one named last changes fastest.
Arguments:
- tensor_low: bfloat16 [16, 256, 256, 256], P('leaf', None, 'leg'), may hold values from -0.0234375 to 0.0234375
- tensor_mid: bfloat16 [16, 256, 128, 256], P('leaf', None, 'leg'), may hold values from -0.0234375 to 0.0234375
- tensor_top: bfloat16 [16, 256, 64, 256], P('leaf', None, 'leg'), may hold values from -0.0234375 to 0.0234375
- child_operators: bfloat16 [16, 2, 4, 256, 256], P('leaf'), may hold values from -6 to 6
- term_choice: int32 [16, 2, 2], P('leaf'), may hold values from 0 to 3
Outputs:
- top_operators: float32 [16, 2, 64, 256], P('leaf', None, 'leg')
All inputs are finite; a program needn't handle non-finite values.
Results may differ from a plain program's by a relative error of at most 0.019.
Values may be sent and summed in bfloat16 or wider, within the bound.
A program may use at most 64 MiB of HBM per device.

v0:
```python
import jax
import jax.numpy as jnp
from jax import lax
from jax.sharding import PartitionSpec as P


def from_partner(block, axis, apart):
    count = lax.axis_size(axis)
    route = []
    for low in range(count):
        high = low | 1 << apart
        if high != low and high < count:
            route += [(low, high), (high, low)]
    return lax.ppermute(block, axis, route)


def filled_up(lines, length):
    spare = -len(lines) % length
    return jnp.pad(lines, [(0, spare)] + [(0, 0)] * (lines.ndim - 1))


def sent_to_all(shard, axis):
    copies = jnp.broadcast_to(shard, (lax.axis_size(axis), *shard.shape))
    return lax.all_to_all(copies, axis, split_axis=0, concat_axis=0, tiled=True)


def joined_along(pieces, dim):
    pieces = jnp.moveaxis(pieces, 0, dim)
    lengths = pieces.shape
    return pieces.reshape(*lengths[:dim], lengths[dim] * lengths[dim + 1], *lengths[dim + 2 :])


def collect(shard, axis, dim):
    pieces = sent_to_all(shard, axis)
    return joined_along(pieces, dim)


def in_blocks(shard, dim, length):
    lengths = shard.shape
    pieces = shard.reshape(*lengths[:dim], length, lengths[dim] // length, *lengths[dim + 1 :])
    return jnp.moveaxis(pieces, dim, 0)


def sent_and_summed(shard, axis, dim):
    pieces = in_blocks(shard, dim, lax.axis_size(axis))
    arrived = lax.all_to_all(pieces, axis, split_axis=0, concat_axis=0, tiled=True)
    return arrived.sum(axis=0)


def sum_by_parts(shard, axes):
    lines = shard.reshape(-1, shard.shape[-1])
    padded = filled_up(lines, lax.axis_size(axes))
    whole = collect(sent_and_summed(padded, axes, 0), axes, 0)
    return lax.slice_in_dim(whole, 0, len(lines)).reshape(shard.shape)


def regroup(stacked, leaf_flag_bits, leg_count):
    stacked_count, bond_size, row_count, feature_width = stacked.shape
    group_size = 2 ** len(leaf_flag_bits)
    slice_width = bond_size // (leg_count * group_size)
    shaped = stacked.reshape(
        stacked_count, leg_count, group_size, slice_width, 1, row_count, feature_width
    )
    leaf_index = lax.axis_index("leaf")
    for leaf_bit in leaf_flag_bits:
        own_bit = leaf_index >> leaf_bit & 1
        dims_now = shaped.shape
        halves = shaped.reshape(dims_now[:2] + (2, dims_now[2] // 2) + dims_now[3:])
        kept_half = lax.dynamic_index_in_dim(halves, own_bit, 2, keepdims=False)
        sent_half = lax.dynamic_index_in_dim(halves, 1 - own_bit, 2, keepdims=False)
        partner = from_partner(sent_half, "leaf", leaf_bit)
        lower_half = jnp.where(own_bit == 0, kept_half, partner)
        upper_half = jnp.where(own_bit == 0, partner, kept_half)
        joined = jnp.stack([lower_half, upper_half], axis=5)
        shaped = joined.reshape(
            dims_now[:2] + (dims_now[2] // 2, dims_now[3], dims_now[4] * 2) + dims_now[5:]
        )
    flattened = shaped.reshape(
        stacked_count, leg_count, slice_width, group_size * row_count, feature_width
    )
    regrouped = lax.all_to_all(flattened, "leg", split_axis=1, concat_axis=3, tiled=True)
    return regrouped.reshape(stacked_count, slice_width, bond_size, feature_width)


def contract_left(left_ops, tensor):
    return jnp.einsum("tlm,lra->tmra", left_ops, tensor, preferred_element_type=jnp.float32).astype(
        jnp.bfloat16
    )


def renormalize_level(tensor, left_ops, right_ops, leaf_flag_bits, leg_count):
    shifted_tensor = regroup(tensor[None], leaf_flag_bits, leg_count)[0]
    left_mixed = contract_left(left_ops, tensor)
    mixed_moved = regroup(left_mixed, leaf_flag_bits, leg_count)
    rotated_tensor = jnp.einsum(
        "tkra,trs->tkas", mixed_moved, right_ops, preferred_element_type=jnp.float32
    ).astype(jnp.bfloat16)
    partial_value = jnp.einsum(
        "tkas,ksb->tab", rotated_tensor, shifted_tensor, preferred_element_type=jnp.float32
    )
    totals = sum_by_parts(partial_value, "leg")
    for leaf_bit in leaf_flag_bits:
        totals = totals + from_partner(totals, "leaf", leaf_bit)
    return totals


def join_terms(tensor, term_bit):
    partner = from_partner(tensor, "leaf", 0)
    lower_half = jnp.where(term_bit == 0, tensor, partner)
    upper_half = jnp.where(term_bit == 0, partner, tensor)
    return jnp.concatenate([lower_half, upper_half], axis=1)


def on_device(tensor_low, tensor_mid, tensor_top, child_operators, term_choice):
    leg_count = lax.axis_size("leg")
    leaf_index = lax.axis_index("leaf")
    operator_bank = child_operators[0]
    chosen_operators = term_choice[0]
    left_ops = jnp.stack(
        [
            lax.dynamic_index_in_dim(
                operator_bank[0], chosen_operators[term_index, 0], 0, keepdims=False
            )
            for term_index in range(2)
        ]
    )
    right_ops = jnp.stack(
        [
            lax.dynamic_index_in_dim(
                operator_bank[1], chosen_operators[term_index, 1], 0, keepdims=False
            )
            for term_index in range(2)
        ]
    )
    level_low = renormalize_level(tensor_low[0], left_ops, right_ops, [], leg_count).astype(
        jnp.bfloat16
    )
    bond_size = level_low.shape[-1]
    quarter = bond_size // 4
    row_count = quarter // leg_count
    leg_index = lax.axis_index("leg")
    row_start = (leaf_index & 3) * quarter + leg_index * row_count
    term_bit = leaf_index & 1
    own_term = lax.dynamic_index_in_dim(level_low, term_bit, 0)
    sent_term = lax.dynamic_index_in_dim(level_low, 1 - term_bit, 0)
    partner = from_partner(sent_term, "leaf", 0)
    left_ops = jnp.where(term_bit == 0, own_term, partner)
    right_ops = jnp.where(term_bit == 0, partner, own_term)
    level_mid = renormalize_level(
        join_terms(tensor_mid[0], term_bit), left_ops, right_ops, [], leg_count
    ).astype(jnp.bfloat16)
    side_bit = leaf_index >> 1 & 1
    sibling = from_partner(level_mid, "leaf", 1)
    left_ops = jnp.where(side_bit == 0, level_mid, sibling)
    right_ops = jnp.where(side_bit == 0, sibling, level_mid)
    level_top = renormalize_level(
        join_terms(tensor_top[0], term_bit), left_ops, right_ops, [1], leg_count
    )
    other_start = (leaf_index & 3 ^ 1) * quarter + leg_index * row_count
    own_rows = lax.dynamic_slice_in_dim(level_top, row_start, row_count, 1)
    other_rows = from_partner(
        lax.dynamic_slice_in_dim(level_top, other_start, row_count, 1), "leaf", 0
    )
    top_rows = jnp.where(
        term_bit == 0,
        jnp.concatenate([own_rows, other_rows], 0),
        jnp.concatenate([other_rows, own_rows], 0),
    )
    return top_rows[None]


def solution(mesh):
    return jax.shard_map(
        on_device,
        mesh=mesh,
        in_specs=(
            P("leaf", None, "leg", None),
            P("leaf", None, "leg", None),
            P("leaf", None, "leg", None),
            P("leaf", None, None, None, None),
            P("leaf", None, None),
        ),
        out_specs=P("leaf", None, "leg", None),
        check_vma=False,
    )
```

profile of v0, /device:TPU:1, one launch (start us, length us, event | category | flops | bytes accessed | tf_op | source)
XLA Modules:
  0.0 323.5 jit_solution(15551411559564682658)
XLA Ops:
  0.0 7.8 %all-to-all-start.1 = ((bf16[1,16,16,16,256]{4,3,2,0,1:T(8,128)(2,1)}), bf16[1,16,16,16,256]{4,3,2,0,1:T(8,128)(2,1)}, u32[]{:S(2)}, u32[]{:S(2)}) async-start(bf16[1,16,16,16,256]{4,3,2,0,1:T(8,128)(2,1)} %bitcast.172), calls=%async_computation.1 | async-start | bytes 4194304 | tf_op jit(solution)/shard_map/all_to_all | solution.py:81
  15.1 5.4 %copy.72 = bf16[2,16,16,16,256]{4,3,2,0,1:T(8,128)(2,1)} copy(bf16[2,16,16,16,256]{4,2,1,3,0:T(8,128)(2,1)S(1)} %bitcast.171) | data formatting | bytes 8388608 | tf_op jit(solution)/shard_map/reshape;reshape | solution.py:78
  20.5 18.2 %all-to-all-done.1 = bf16[1,16,16,16,256]{4,3,2,0,1:T(8,128)(2,1)} async-done(((bf16[1,16,16,16,256]{4,3,2,0,1:T(8,128)(2,1)}), bf16[1,16,16,16,256]{4,3,2,0,1:T(8,128)(2,1)}, u32[]{:S(2)}, u32[]{:S(2)}) %all-to-all-start.1) | async-done | bytes 2097184 | tf_op jit(solution)/shard_map/all_to_all | solution.py:81
  38.8 4.5 %all-to-all-start = ((bf16[2,16,16,16,256]{4,3,2,0,1:T(8,128)(2,1)}), bf16[2,16,16,16,256]{4,3,2,0,1:T(8,128)(2,1)}, u32[]{:S(2)}, u32[]{:S(2)}) async-start(bf16[2,16,16,16,256]{4,3,2,0,1:T(8,128)(2,1)} %copy.72), calls=%async_computation | async-start | bytes 8388608 | tf_op jit(solution)/shard_map/all_to_all | solution.py:81
  52.1 51.3 %all-to-all-done = bf16[2,16,16,16,256]{4,3,2,0,1:T(8,128)(2,1)} async-done(((bf16[2,16,16,16,256]{4,3,2,0,1:T(8,128)(2,1)}), bf16[2,16,16,16,256]{4,3,2,0,1:T(8,128)(2,1)}, u32[]{:S(2)}, u32[]{:S(2)}) %all-to-all-start) | async-done | bytes 4194336 | tf_op jit(solution)/shard_map/all_to_all | solution.py:81
  113.5 4.3 %all-to-all-start.2 = ((f32[16,32,256]{2,1,0:T(8,128)}), f32[16,32,256]{2,1,0:T(8,128)S(1)}, u32[]{:S(2)}, u32[]{:S(2)}) async-start(f32[16,32,256]{2,1,0:T(8,128)} %fusion.4), calls=%async_computation.2 | async-start | bytes 1048576 | tf_op jit(solution)/shard_map/all_to_all | solution.py:46
  117.9 9.0 %all-to-all-done.2 = f32[16,32,256]{2,1,0:T(8,128)S(1)} async-done(((f32[16,32,256]{2,1,0:T(8,128)}), f32[16,32,256]{2,1,0:T(8,128)S(1)}, u32[]{:S(2)}, u32[]{:S(2)}) %all-to-all-start.2) | async-done | bytes 524320 | tf_op jit(solution)/shard_map/all_to_all | solution.py:46
  138.7 3.7 %all-to-all-start.5 = ((bf16[1,16,16,16,256]{4,2,3,0,1:T(8,128)(2,1)}), bf16[1,16,16,16,256]{4,2,3,0,1:T(8,128)(2,1)S(1)}, u32[]{:S(2)}, u32[]{:S(2)}) async-start(bf16[1,16,16,16,256]{4,2,3,0,1:T(8,128)(2,1)} %copy.83), calls=%async_computation.5 | async-start | bytes 4194304 | tf_op jit(solution)/shard_map/all_to_all | solution.py:81
  143.1 5.2 %collective-permute-start = (bf16[1,256,256]{2,1,0:T(8,128)(2,1)}, bf16[1,256,256]{2,1,0:T(8,128)(2,1)S(1)}, u32[]{:S(2)}, u32[]{:S(2)}) collective-permute-start(bf16[1,256,256]{2,1,0:T(8,128)(2,1)} %constant_dynamic-slice_fusion.5), channel_id=1, source_target_pairs={{0,16},{16,0},{32,48},{48,32},{64,80},{80,64},{96,112},{112,96},{1... | collective-permute-start | bytes 393224 | tf_op jit(solution)/shard_map/ppermute | solution.py:14
  153.9 12.7 %all-to-all-done.5 = bf16[1,16,16,16,256]{4,2,3,0,1:T(8,128)(2,1)S(1)} async-done(((bf16[1,16,16,16,256]{4,2,3,0,1:T(8,128)(2,1)}), bf16[1,16,16,16,256]{4,2,3,0,1:T(8,128)(2,1)S(1)}, u32[]{:S(2)}, u32[]{:S(2)}) %all-to-all-start.5) | async-done | bytes 2097184 | tf_op jit(solution)/shard_map/all_to_all | solution.py:81
  166.6 6.2 %all-to-all-start.4 = ((bf16[1,16,16,16,256]{4,3,2,0,1:T(8,128)(2,1)}), bf16[1,16,16,16,256]{4,3,2,0,1:T(8,128)(2,1)}, u32[]{:S(2)}, u32[]{:S(2)}) async-start(bf16[1,16,16,16,256]{4,3,2,0,1:T(8,128)(2,1)} %copy.80), calls=%async_computation.4 | async-start | bytes 4194304 | tf_op jit(solution)/shard_map/all_to_all | solution.py:81
  173.6 5.8 %collective-permute-start.3 = (bf16[256,4,256]{2,0,1:T(8,128)(2,1)}, bf16[256,4,256]{2,0,1:T(8,128)(2,1)S(1)}, u32[]{:S(2)}, u32[]{:S(2)}) collective-permute-start(bf16[256,4,256]{2,0,1:T(8,128)(2,1)} %bitcast.168), channel_id=1, source_target_pairs={{0,16},{16,0},{32,48},{48,32},{64,80},{80,64},{96,112},{112,96},{1... | collective-permute-start | bytes 1572872 | tf_op jit(solution)/shard_map/ppermute | solution.py:14
  181.5 15.4 %all-to-all-done.4 = bf16[1,16,16,16,256]{4,3,2,0,1:T(8,128)(2,1)} async-done(((bf16[1,16,16,16,256]{4,3,2,0,1:T(8,128)(2,1)}), bf16[1,16,16,16,256]{4,3,2,0,1:T(8,128)(2,1)}, u32[]{:S(2)}, u32[]{:S(2)}) %all-to-all-start.4) | async-done | bytes 2097184 | tf_op jit(solution)/shard_map/all_to_all | solution.py:81
  201.7 4.9 %all-to-all-start.6 = ((f32[16,16,256]{2,1,0:T(8,128)}), f32[16,16,256]{2,1,0:T(8,128)S(1)}, u32[]{:S(2)}, u32[]{:S(2)}) async-start(f32[16,16,256]{2,1,0:T(8,128)} %convolution_bitcast_fusion.1), calls=%async_computation.6 | async-start | bytes 524288 | tf_op jit(solution)/shard_map/all_to_all | solution.py:46
  206.6 7.5 %all-to-all-done.6 = f32[16,16,256]{2,1,0:T(8,128)S(1)} async-done(((f32[16,16,256]{2,1,0:T(8,128)}), f32[16,16,256]{2,1,0:T(8,128)S(1)}, u32[]{:S(2)}, u32[]{:S(2)}) %all-to-all-start.6) | async-done | bytes 262176 | tf_op jit(solution)/shard_map/all_to_all | solution.py:46
  218.5 6.7 %all-to-all-done.7 = bf16[16,16,256]{2,1,0:T(8,128)(2,1)S(1)} async-done(((bf16[16,16,256]{2,1,0:T(8,128)(2,1)}), bf16[16,16,256]{2,1,0:T(8,128)(2,1)S(1)}, u32[]{:S(2)}, u32[]{:S(2)}) %all-to-all-start.7) | async-done | bytes 131104 | tf_op jit(solution)/shard_map/all_to_all | solution.py:24
  231.8 8.0 %collective-permute-done.5 = bf16[1,16,1,8,1,8,256]{6,5,3,1,4,2,0:T(8,128)(2,1)S(1)} collective-permute-done((bf16[1,16,1,8,1,8,256]{6,5,3,1,4,2,0:T(8,128)(2,1)S(1)}, bf16[1,16,1,8,1,8,256]{6,5,3,1,4,2,0:T(8,128)(2,1)S(1)}, u32[]{:S(2)}, u32[]{:S(2)}) %collective-permute-start.5) | collective-permute-done | bytes 524320 | tf_op jit(solution)/shard_map/ppermute | solution.py:14
  246.8 8.4 %collective-permute-done.4 = bf16[1,16,1,8,1,8,256]{6,5,3,1,4,2,0:T(8,128)(2,1)S(1)} collective-permute-done((bf16[1,16,1,8,1,8,256]{6,5,3,1,4,2,0:T(8,128)(2,1)S(1)}, bf16[1,16,1,8,1,8,256]{6,5,3,1,4,2,0:T(8,128)(2,1)S(1)}, u32[]{:S(2)}, u32[]{:S(2)}) %collective-permute-start.4) | collective-permute-done | bytes 524320 | tf_op jit(solution)/shard_map/ppermute | solution.py:14
  257.0 4.4 %all-to-all-start.8 = ((bf16[1,16,8,16,256]{4,3,2,0,1:T(8,128)(2,1)}), bf16[1,16,8,16,256]{4,3,2,0,1:T(8,128)(2,1)S(1)}, u32[]{:S(2)}, u32[]{:S(2)}) async-start(bf16[1,16,8,16,256]{4,3,2,0,1:T(8,128)(2,1)} %maximum_bitcast_fusion), calls=%async_computation.8 | async-start | bytes 2097152 | tf_op jit(solution)/shard_map/all_to_all | solution.py:81
  261.4 14.0 %all-to-all-done.8 = bf16[1,16,8,16,256]{4,3,2,0,1:T(8,128)(2,1)S(1)} async-done(((bf16[1,16,8,16,256]{4,3,2,0,1:T(8,128)(2,1)}), bf16[1,16,8,16,256]{4,3,2,0,1:T(8,128)(2,1)S(1)}, u32[]{:S(2)}, u32[]{:S(2)}) %all-to-all-start.8) | async-done | bytes 1048608 | tf_op jit(solution)/shard_map/all_to_all | solution.py:81
  276.5 11.7 %all_to_all.120 = f32[16,16,256]{2,1,0:T(8,128)S(1)} all-to-all(f32[16,16,256]{2,1,0:T(8,128)S(1)} %convolution_bitcast_fusion), channel_id=1, replica_groups=mesh['leaf'=16,'leg'=16] {'leg'}, dimensions={0} | all-to-all | bytes 524288 | tf_op jit(solution)/shard_map/all_to_all | solution.py:46
  288.3 11.2 %all_to_all.121 = f32[16,16,256]{2,1,0:T(8,128)S(1)} all-to-all(f32[16,16,256]{2,1,0:T(8,128)S(1)} %broadcast_in_dim.12), channel_id=1, replica_groups=mesh['leaf'=16,'leg'=16] {'leg'}, dimensions={0} | all-to-all | bytes 524288 | tf_op jit(solution)/shard_map/all_to_all | solution.py:24
  301.5 3.8 %collective-permute-done.6 = f32[1,256,256]{2,1,0:T(8,128)S(1)} collective-permute-done((f32[1,256,256]{2,1,0:T(8,128)S(1)}, f32[1,256,256]{2,1,0:T(8,128)S(1)}, u32[]{:S(2)}, u32[]{:S(2)}) %collective-permute-start.6) | collective-permute-done | bytes 262176 | tf_op jit(solution)/shard_map/ppermute | solution.py:14
  305.3 16.8 %collective-permute-start.7 = (f32[1,4,256]{2,1,0:T(4,128)S(1)}, f32[1,4,256]{2,1,0:T(4,128)S(1)}, u32[]{:S(2)}, u32[]{:S(2)}) collective-permute-start(f32[1,4,256]{2,1,0:T(4,128)S(1)} %get-tuple-element.24), channel_id=1, source_target_pairs={{0,16},{16,0},{32,48},{48,32},{64,80},{80,64},{96,112},{112,96},{1... | collective-permute-start | bytes 12296 | tf_op jit(solution)/shard_map/ppermute | solution.py:14
  (74 shorter events, 68.5 us)
Async XLA Ops:
  0.0 7.8 %copy-start.5 = (s32[1,2,2]{2,1,0:T(2,128)S(1)}, s32[1,2,2]{2,1,0:T(2,128)}, u32[]{:S(2)}) copy-start(s32[1,2,2]{2,1,0:T(2,128)} %param.9) | copy-start | bytes 52
  0.0 38.8 %all-to-all-start.1 = ((bf16[1,16,16,16,256]{4,3,2,0,1:T(8,128)(2,1)}), bf16[1,16,16,16,256]{4,3,2,0,1:T(8,128)(2,1)}, u32[]{:S(2)}, u32[]{:S(2)}) async-start(bf16[1,16,16,16,256]{4,3,2,0,1:T(8,128)(2,1)} %bitcast.172), calls=%async_computation.1 | async-start | bytes 4194304 | tf_op jit(solution)/shard_map/all_to_all | solution.py:81
  7.8 6.0 %copy-start = (bf16[1,256,16,256]{3,2,1,0:T(8,128)(2,1)S(1)}, bf16[1,256,16,256]{3,2,1,0:T(8,128)(2,1)}, u32[]{:S(2)}) copy-start(bf16[1,256,16,256]{3,2,1,0:T(8,128)(2,1)} %param.5) | copy-start | bytes 6291460
  20.5 22.8 %copy-start.2 = (bf16[1,256,8,256]{3,2,1,0:T(8,128)(2,1)S(1)}, bf16[1,256,8,256]{3,2,1,0:T(8,128)(2,1)}, u32[]{:S(2)}) copy-start(bf16[1,256,8,256]{3,2,1,0:T(8,128)(2,1)} %param.6) | copy-start | bytes 3145732
  38.8 64.7 %all-to-all-start = ((bf16[2,16,16,16,256]{4,3,2,0,1:T(8,128)(2,1)}), bf16[2,16,16,16,256]{4,3,2,0,1:T(8,128)(2,1)}, u32[]{:S(2)}, u32[]{:S(2)}) async-start(bf16[2,16,16,16,256]{4,3,2,0,1:T(8,128)(2,1)} %copy.72), calls=%async_computation | async-start | bytes 8388608 | tf_op jit(solution)/shard_map/all_to_all | solution.py:81
  44.5 86.6 %collective-permute-start.1 = (bf16[256,8,256]{2,0,1:T(8,128)(2,1)}, bf16[256,8,256]{2,0,1:T(8,128)(2,1)}, u32[]{:S(2)}, u32[]{:S(2)}) collective-permute-start(bf16[256,8,256]{2,0,1:T(8,128)(2,1)} %bitcast.165), channel_id=1, source_target_pairs={{0,16},{16,0},{32,48},{48,32},{64,80},{80,64},{96,112},{112,96},{1... | collective-permute-start | bytes 3145736 | tf_op jit(solution)/shard_map/ppermute | solution.py:14
  113.5 13.3 %all-to-all-start.2 = ((f32[16,32,256]{2,1,0:T(8,128)}), f32[16,32,256]{2,1,0:T(8,128)S(1)}, u32[]{:S(2)}, u32[]{:S(2)}) async-start(f32[16,32,256]{2,1,0:T(8,128)} %fusion.4), calls=%async_computation.2 | async-start | bytes 1048576 | tf_op jit(solution)/shard_map/all_to_all | solution.py:46
  127.6 11.0 %all-to-all-start.3 = ((bf16[16,32,256]{2,1,0:T(8,128)(2,1)}), bf16[16,32,256]{2,1,0:T(8,128)(2,1)S(1)}, u32[]{:S(2)}, u32[]{:S(2)}) async-start(bf16[16,32,256]{2,1,0:T(8,128)(2,1)} %broadcast_in_dim.10), calls=%async_computation.3 | async-start | bytes 524288 | tf_op jit(solution)/shard_map/all_to_all | solution.py:24
  132.6 1.0 copy-start.3
  138.7 27.9 %all-to-all-start.5 = ((bf16[1,16,16,16,256]{4,2,3,0,1:T(8,128)(2,1)}), bf16[1,16,16,16,256]{4,2,3,0,1:T(8,128)(2,1)S(1)}, u32[]{:S(2)}, u32[]{:S(2)}) async-start(bf16[1,16,16,16,256]{4,2,3,0,1:T(8,128)(2,1)} %copy.83), calls=%async_computation.5 | async-start | bytes 4194304 | tf_op jit(solution)/shard_map/all_to_all | solution.py:81
  143.1 6.4 %collective-permute-start = (bf16[1,256,256]{2,1,0:T(8,128)(2,1)}, bf16[1,256,256]{2,1,0:T(8,128)(2,1)S(1)}, u32[]{:S(2)}, u32[]{:S(2)}) collective-permute-start(bf16[1,256,256]{2,1,0:T(8,128)(2,1)} %constant_dynamic-slice_fusion.5), channel_id=1, source_target_pairs={{0,16},{16,0},{32,48},{48,32},{64,80},{80,64},{96,112},{112,96},{1... | collective-permute-start | bytes 393224 | tf_op jit(solution)/shard_map/ppermute | solution.py:14
  153.9 18.8 %copy-start.4 = (bf16[1,256,4,256]{3,2,1,0:T(4,128)(2,1)S(1)}, bf16[1,256,4,256]{3,2,1,0:T(4,128)(2,1)}, u32[]{:S(2)}) copy-start(bf16[1,256,4,256]{3,2,1,0:T(4,128)(2,1)} %param.7) | copy-start | bytes 1572868
  166.6 30.3 %all-to-all-start.4 = ((bf16[1,16,16,16,256]{4,3,2,0,1:T(8,128)(2,1)}), bf16[1,16,16,16,256]{4,3,2,0,1:T(8,128)(2,1)}, u32[]{:S(2)}, u32[]{:S(2)}) async-start(bf16[1,16,16,16,256]{4,3,2,0,1:T(8,128)(2,1)} %copy.80), calls=%async_computation.4 | async-start | bytes 4194304 | tf_op jit(solution)/shard_map/all_to_all | solution.py:81
  173.6 44.7 %collective-permute-start.3 = (bf16[256,4,256]{2,0,1:T(8,128)(2,1)}, bf16[256,4,256]{2,0,1:T(8,128)(2,1)S(1)}, u32[]{:S(2)}, u32[]{:S(2)}) collective-permute-start(bf16[256,4,256]{2,0,1:T(8,128)(2,1)} %bitcast.168), channel_id=1, source_target_pairs={{0,16},{16,0},{32,48},{48,32},{64,80},{80,64},{96,112},{112,96},{1... | collective-permute-start | bytes 1572872 | tf_op jit(solution)/shard_map/ppermute | solution.py:14
  198.7 1.6 copy-start.1
  201.7 12.4 %all-to-all-start.6 = ((f32[16,16,256]{2,1,0:T(8,128)}), f32[16,16,256]{2,1,0:T(8,128)S(1)}, u32[]{:S(2)}, u32[]{:S(2)}) async-start(f32[16,16,256]{2,1,0:T(8,128)} %convolution_bitcast_fusion.1), calls=%async_computation.6 | async-start | bytes 524288 | tf_op jit(solution)/shard_map/all_to_all | solution.py:46
  214.8 10.3 %all-to-all-start.7 = ((bf16[16,16,256]{2,1,0:T(8,128)(2,1)}), bf16[16,16,256]{2,1,0:T(8,128)(2,1)S(1)}, u32[]{:S(2)}, u32[]{:S(2)}) async-start(bf16[16,16,256]{2,1,0:T(8,128)(2,1)} %broadcast_in_dim.11), calls=%async_computation.7 | async-start | bytes 262144 | tf_op jit(solution)/shard_map/all_to_all | solution.py:24
  225.1 4.0 %collective-permute-start.2 = (bf16[1,256,256]{2,1,0:T(8,128)(2,1)S(1)}, bf16[1,256,256]{2,1,0:T(8,128)(2,1)S(1)}, u32[]{:S(2)}, u32[]{:S(2)}) collective-permute-start(bf16[1,256,256]{2,1,0:T(8,128)(2,1)S(1)} %bitcast.193), channel_id=1, source_target_pairs={{0,32},{32,0},{16,48},{48,16},{64,96},{96,64},{80,112},{112,80},{1... | collective-permute-start | bytes 393224 | tf_op jit(solution)/shard_map/ppermute | solution.py:14
  230.1 9.7 %collective-permute-start.5 = (bf16[1,16,1,8,1,8,256]{6,5,3,1,4,2,0:T(8,128)(2,1)S(1)}, bf16[1,16,1,8,1,8,256]{6,5,3,1,4,2,0:T(8,128)(2,1)S(1)}, u32[]{:S(2)}, u32[]{:S(2)}) collective-permute-start(bf16[1,16,1,8,1,8,256]{6,5,3,1,4,2,0:T(8,128)(2,1)S(1)} %bitcast.198), channel_id=1, source_target_pairs={{0,32},{32,0},{16,48},{48,16},{64,96},{96,64},{80,112},{112,80},{1... | collective-permute-start | bytes 1572872 | tf_op jit(solution)/shard_map/ppermute | solution.py:14
  241.1 15.8 %all-to-all-start.9 = ((bf16[1,16,8,16,256]{4,3,2,0,1:T(8,128)(2,1)}), bf16[1,16,8,16,256]{4,3,2,0,1:T(8,128)(2,1)S(1)}, u32[]{:S(2)}, u32[]{:S(2)}) async-start(bf16[1,16,8,16,256]{4,3,2,0,1:T(8,128)(2,1)} %copy_bitcast_fusion), calls=%async_computation.9 | async-start | bytes 2097152 | tf_op jit(solution)/shard_map/all_to_all | solution.py:81
  245.1 10.1 %collective-permute-start.4 = (bf16[1,16,1,8,1,8,256]{6,5,3,1,4,2,0:T(8,128)(2,1)S(1)}, bf16[1,16,1,8,1,8,256]{6,5,3,1,4,2,0:T(8,128)(2,1)S(1)}, u32[]{:S(2)}, u32[]{:S(2)}) collective-permute-start(bf16[1,16,1,8,1,8,256]{6,5,3,1,4,2,0:T(8,128)(2,1)S(1)} %bitcast.199), channel_id=1, source_target_pairs={{0,32},{32,0},{16,48},{48,16},{64,96},{96,64},{80,112},{112,80},{1... | collective-permute-start | bytes 1572872 | tf_op jit(solution)/shard_map/ppermute | solution.py:14
  257.0 18.5 %all-to-all-start.8 = ((bf16[1,16,8,16,256]{4,3,2,0,1:T(8,128)(2,1)}), bf16[1,16,8,16,256]{4,3,2,0,1:T(8,128)(2,1)S(1)}, u32[]{:S(2)}, u32[]{:S(2)}) async-start(bf16[1,16,8,16,256]{4,3,2,0,1:T(8,128)(2,1)} %maximum_bitcast_fusion), calls=%async_computation.8 | async-start | bytes 2097152 | tf_op jit(solution)/shard_map/all_to_all | solution.py:81
  299.5 5.8 %collective-permute-start.6 = (f32[1,256,256]{2,1,0:T(8,128)S(1)}, f32[1,256,256]{2,1,0:T(8,128)S(1)}, u32[]{:S(2)}, u32[]{:S(2)}) collective-permute-start(f32[1,256,256]{2,1,0:T(8,128)S(1)} %bitcast.188), channel_id=1, source_target_pairs={{0,32},{32,0},{16,48},{48,16},{64,96},{96,64},{80,112},{112,80},{1... | collective-permute-start | bytes 786440 | tf_op jit(solution)/shard_map/ppermute | solution.py:14
  305.3 17.6 %collective-permute-start.7 = (f32[1,4,256]{2,1,0:T(4,128)S(1)}, f32[1,4,256]{2,1,0:T(4,128)S(1)}, u32[]{:S(2)}, u32[]{:S(2)}) collective-permute-start(f32[1,4,256]{2,1,0:T(4,128)S(1)} %get-tuple-element.24), channel_id=1, source_target_pairs={{0,16},{16,0},{32,48},{48,32},{64,80},{80,64},{96,112},{112,96},{1... | collective-permute-start | bytes 12296 | tf_op jit(solution)/shard_map/ppermute | solution.py:14
where the time goes:
time: 325 us; the launch traced here: 324 us
  waiting for transfers between devices  163 us (50%)
  starting transfers between devices  82.9 us (26%)
  local copies, waits for them, and re-layouts  29.2 us (9%)
  blocking collectives  22.9 us (7%)
  matrix products  11.8 us (4%)
  between operations  8.16 us (3%)
  other arithmetic  5.35 us (2%)
    all_to_all x6, waiting for transfers between devices, regroup(): lax.all_to_all(flattened, 'leg', split_axis=1, concat_axis=3, tiled=True)  112 us
    ppermute x8, starting transfers between devices, from_partner(): return lax.ppermute(block, axis, route)  36.5 us
    all_to_all x6, starting transfers between devices, regroup(): lax.all_to_all(flattened, 'leg', split_axis=1, concat_axis=3, tiled=True)  30.2 us
    ppermute x8, waiting for transfers between devices, from_partner(): return lax.ppermute(block, axis, route)  24.5 us
    all_to_all x2, waiting for transfers between devices, sent_and_summed(): lax.all_to_all(pieces, axis, split_axis=0, concat_axis=0, tiled=True)  16.5 us
    all_to_all x1, blocking collectives, sent_and_summed(): lax.all_to_all(pieces, axis, split_axis=0, concat_axis=0, tiled=True)  11.7 us
    all_to_all x1, blocking collectives, sent_to_all(): return lax.all_to_all(copies, axis, split_axis=0, concat_axis=0, tiled=True)  11.2 us
    all_to_all x2, waiting for transfers between devices, sent_to_all(): return lax.all_to_all(copies, axis, split_axis=0, concat_axis=0, tiled=True)  10.2 us
  transfers between devices with their start and end apart: 18, of which 16 were waited for; matrix products, arithmetic and copies ran while one was open for 13% of the time, Pallas kernels for 0%

commit v1 on v0

v1 whole, which is shorter than its diff:
```python
import jax
import jax.numpy as jnp
from jax import lax
from jax.experimental import pallas as pl
from jax.experimental.pallas import tpu as pltpu
from jax.sharding import PartitionSpec as P

BF, F32 = jnp.bfloat16, jnp.float32
MESH = pl.DeviceIdType.MESH
BOND = 256
LEGS = 16


def x_near(leg):
    x = leg % 4
    return leg // 4 * 4 + x + 1 - 2 * (x % 2)


def x_far(leg):
    return leg // 4 * 4 + 3 - leg % 4


def y_near(leg):
    y = leg // 4
    return (y + 1 - 2 * (y % 2)) * 4 + leg % 4


def y_far(leg):
    return (3 - leg // 4) * 4 + leg % 4


def pick(core, first, second):
    return first + (second - first) * core


def rows_at(start, size):
    return pl.ds(pl.multiple_of(start, 8), size)


class Level:
    def __init__(self, env, ws, wl, sems, own_rows, own_at, left_bits, gather, spread, halves):
        self.env, self.ws, self.wl = env, ws, wl
        self.a_sem, self.b1_sem, self.bd_sem, self.br_sem, self.loc_sem, self.share_sem = sems
        self.own_rows, self.own_at = own_rows, own_at
        self.n_left = own_rows // 4
        self.left_at = own_at + left_bits * self.n_left
        self.halves, self.part = halves, 16 // halves
        core, leg = env["core"], env["leg"]
        fx, fy = gather
        gx, gy = spread
        self.slot_legs = [leg, fx(leg), fy(leg), fx(fy(leg))]
        self.a1 = pick(core, fx(leg), fy(leg))
        self.a2 = pick(core, fy(leg), fx(leg))
        self.first, self.second = 1 + core, 2 - core
        self.b1 = lambda one: pick(core, gy(one), gx(one))
        self.b2 = lambda one: pick(core, gx(one), gy(one))
        self.leg_of = {"own": leg, "first": self.a1, "second": self.a2, "both": fx(fy(leg))}
        self.slot_of = {"own": 0, "first": self.first, "second": self.second, "both": 3}
        self.pending = []

    def remote(self, src, dst, sem, index, to):
        return pltpu.make_async_remote_copy(
            src_ref=src,
            dst_ref=dst,
            send_sem=sem.at[(0, *index)],
            recv_sem=sem.at[(1, *index)],
            device_id=to,
            device_id_type=MESH,
        )

    def go(self, copy):
        copy.start()
        self.pending.append(copy)

    def block(self, slot, h):
        return self.ws.at[
            slot, rows_at(self.own_at, self.own_rows), pl.ds(h * self.part, self.part), :
        ]

    def piece(self, slot, h):
        return self.ws.at[
            slot, rows_at(self.left_at, self.n_left), pl.ds(h * self.part, self.part), :
        ]

    def place(self, one, h):
        return self.wl.at[:, rows_at(one * 16 + h * self.part, self.part), :]

    def to(self, one):
        return (self.env["leaf"], one)

    def hop(self, kind, h, arriving):
        src = {"a1": 0, "own": 0, "relay": self.first}[kind]
        dst = {"a1": self.first, "own": self.second, "relay": 3}[kind]
        target = self.a1 if kind == "a1" else self.a2
        index = ({"a1": 0, "own": 1, "relay": 2}[kind], h)
        source = self.block(dst if arriving else src, h)
        return self.remote(source, self.block(dst, h), self.a_sem, index, self.to(target))

    def send_hop(self, kind, h):
        self.go(self.hop(kind, h, False))

    def recv_hop(self, kind, h):
        self.hop(kind, h, True).wait_recv()

    def spread(self, name, h):
        slot, one = self.slot_of[name], self.leg_of[name]
        piece, place, leg = self.piece(slot, h), self.place(one, h), self.env["leg"]
        self.go(self.remote(piece, place, self.b1_sem, (slot, h), self.to(self.b1(leg))))
        self.go(self.remote(piece, place, self.bd_sem, (slot, h), self.to(self.b2(leg))))
        copy = pltpu.make_async_copy(piece, place, self.loc_sem.at[slot, h])
        copy.start()
        self.pending.append(copy)

    def relay(self, name, h):
        slot, leg = self.slot_of[name], self.env["leg"]
        place = self.place(self.b1(self.leg_of[name]), h)
        self.remote(place, place, self.b1_sem, (slot, h), self.to(self.b1(leg))).wait_recv()
        self.go(self.remote(place, place, self.br_sem, (slot, h), self.to(self.b2(leg))))

    def arrive(self, name, h):
        slot, leg, one = self.slot_of[name], self.env["leg"], self.leg_of[name]
        place = self.place(self.b2(one), h)
        self.remote(place, place, self.bd_sem, (slot, h), self.to(self.b2(leg))).wait_recv()
        place = self.place(self.b2(self.b1(one)), h)
        self.remote(place, place, self.br_sem, (slot, h), self.to(self.b2(leg))).wait_recv()

    def finish(self):
        for copy in self.pending:
            if copy.is_remote:
                copy.wait_send()

    def finish_local(self):
        for copy in self.pending:
            if not copy.is_remote:
                copy.wait()

    def share(self, name, step, start, size, to):
        slot = self.slot_of[name]
        span = self.ws.at[slot, rows_at(start, size)]
        self.go(self.remote(span, span, self.share_sem, (step, slot), to))

    def shared(self, name, step, start, size, to):
        slot = self.slot_of[name]
        span = self.ws.at[slot, rows_at(start, size)]
        self.remote(span, span, self.share_sem, (step, slot), to).wait_recv()


def transfer(src, dst, sem, index, to):
    return pltpu.make_async_remote_copy(
        src_ref=src,
        dst_ref=dst,
        send_sem=sem.at[(0, *index)],
        recv_sem=sem.at[(1, *index)],
        device_id=to,
        device_id_type=MESH,
    )


def kernel(
    w_low, w_mid, w_top, left_in, right_in, out,
    ws_low, ws_mid, ws_top, wl_low, wl_mid, wl_top, top_parts, flat_0, flat_1, ys_0, ys_1, zs, acc, l_cat, r_cat,
    right_t, sums, inbox, block, ops_a, mate_in, mid_sum, mid_in, mid_block, ops_b,
    low_a, low_b1, low_bd, low_br, low_loc, low_share,
    mid_a, mid_b1, mid_bd, mid_br, mid_loc, mid_share,
    top_a, top_b1, top_bd, top_br, top_loc, top_share,
    first_sem, mid_first, top_first, rs_sem, ag_sem, op_sem,
    mate_sem, rs2_sem, ag2_sem, op2_sem, half_sem, quarter_sem, rs3_sem,
    half_in, half_sum, quarter_in, rows_out, rows_in,
):
    leaf, leg = lax.axis_index("leaf"), lax.axis_index("leg")
    core, z = leaf % 2, leaf // 2
    side = z % 2
    x, y = leg % 4, leg // 4
    far_x, far_y = x // 2, y // 2
    near_x, near_y = (x + far_x) % 2, (y + far_y) % 2
    mate = (leaf + 1 - 2 * core, leg)
    across = (leaf + 2 - 4 * side, leg)
    cross = (leaf + 2 - 4 * side + 1 - 2 * core, leg)
    env = {"leaf": leaf, "leg": leg, "core": core}

    barrier = pltpu.get_barrier_semaphore()

    @pl.loop(1, LEGS)
    def _(d):
        pl.semaphore_signal(barrier, inc=1, device_id=(leaf, (leg + d) % LEGS), device_id_type=MESH)

    for peer in (mate, across, cross):
        pl.semaphore_signal(barrier, inc=1, device_id=peer, device_id_type=MESH)
    pl.semaphore_wait(barrier, LEGS + 2)

    low = Level(
        env, ws_low, wl_low, (low_a, low_b1, low_bd, low_br, low_loc, low_share),
        256, 0, near_x + 2 * near_y, (x_near, y_near), (x_far, y_far), 2,
    )
    mid = Level(
        env, ws_mid, wl_mid, (mid_a, mid_b1, mid_bd, mid_br, mid_loc, mid_share),
        128, core * 128, far_x + 2 * far_y, (x_far, y_far), (x_near, y_near), 1,
    )
    top = Level(
        env, ws_top, wl_top, (top_a, top_b1, top_bd, top_br, top_loc, top_share),
        64, core * 128 + side * 64, near_x + 2 * near_y, (x_near, y_near), (x_far, y_far), 1,
    )

    own_low = pltpu.make_async_copy(w_low, ws_low.at[0], first_sem.at[0])
    own_low.start()
    mine = pl.ds(pl.multiple_of(core * 8, 8), 8)
    theirs = pl.ds(pl.multiple_of(8 - core * 8, 8), 8)
    mid_rows, mate_rows = rows_at(core * 128, 128), rows_at(128 - core * 128, 128)
    mid_out = transfer(
        w_mid.at[mate_rows], ws_mid.at[0, mate_rows, mine, :], mid_first, (0,), mate
    )
    mid_out.start()
    own_mid = pltpu.make_async_copy(
        w_mid.at[mid_rows], ws_mid.at[0, mid_rows, mine, :], first_sem.at[1]
    )
    own_mid.start()
    q = side * 2 + core
    quarters = [
        ((1 - core) * 128 + side * 64, side * 2 + 1 - core, mate),
        (core * 128 + (1 - side) * 64, (1 - side) * 2 + core, across),
        ((1 - core) * 128 + (1 - side) * 64, (1 - side) * 2 + 1 - core, cross),
    ]
    top_sends = []
    for n, (start, _, peer) in enumerate(quarters):
        copy = transfer(w_top.at[rows_at(start, 64)], top_parts.at[q], top_first, (n,), peer)
        copy.start()
        top_sends.append(copy)
    own_top = pltpu.make_async_copy(
        w_top.at[rows_at(top.own_at, 64)], top_parts.at[q], first_sem.at[2]
    )
    own_top.start()

    def load_left(ref, n_left, at):
        for t in range(2):
            l_cat[t * n_left : (t + 1) * n_left] = ref[t, rows_at(at, n_left), :]

    def load_right(ref, legs):
        for t in range(2):
            for slot, one in enumerate(legs):
                start = t * 64 + slot * 16
                r_cat[start : start + 16] = ref[t, rows_at(one * 16, 16), :]

    def mix_left(level, name):
        slot, n_left = level.slot_of[name], level.n_left

        @pl.loop(0, 16)
        def _(n):
            rows = level.ws[slot, pl.ds(n * 16, 16), :, :]
            rows = rows.reshape(256, BOND).astype(F32)
            for n_col, ref in enumerate((flat_0, flat_1)):
                ref[pl.ds(n * 256, 256), :] = rows[:, n_col * 128 : n_col * 128 + 128]

        left = l_cat[: 2 * n_left]

        @pl.loop(0, 16)
        def _(s):
            for source, target in ((flat_0, ys_0), (flat_1, ys_1)):
                rows = source[pl.ds(s, 256, stride=16), :].astype(BF)
                target[pl.ds(slot * 16 + s, 2 * n_left, stride=64), :] = jnp.dot(
                    left, rows, preferred_element_type=F32
                )

    def contract(level):
        acc[...] = jnp.zeros_like(acc)
        n_left = level.n_left

        @pl.loop(0, n_left // 4)
        def _(n):
            for k in range(4):
                turned = jnp.dot(
                    r_cat[...], level.wl[n * 4 + k], preferred_element_type=F32
                ).astype(BF)
                for t in range(2):
                    zs[t, k * 64 : (k + 1) * 64] = turned[t * 64 : (t + 1) * 64]
            for t in range(2):
                span = rows_at((t * n_left + n * 4) * 64, 256)
                rows = jnp.concatenate([ys_0[span, :], ys_1[span, :]], axis=1).astype(BF)
                acc[t] += lax.dot_general(
                    zs[t], rows, (((0,), (0,)), ((), ())), preferred_element_type=F32
                )

    def ring_start(src_of, dst_of, sem):
        @pl.loop(1, LEGS)
        def _(d):
            one = (leg + d) % LEGS
            transfer(src_of(one), dst_of(d), sem, (d,), (leaf, one)).start()

    def ring_recv(dst_of, sem):
        @pl.loop(1, LEGS)
        def _(d):
            ref = dst_of(d)
            transfer(ref, ref, sem, (d,), (leaf, (leg + d) % LEGS)).wait_recv()

    def ring_sent(src_of, sem):
        @pl.loop(1, LEGS)
        def _(d):
            one = (leg + d) % LEGS
            ref = src_of(one)
            transfer(ref, ref, sem, (d,), (leaf, one)).wait_send()

    load_left(left_in, low.n_left, low.left_at)
    load_right(right_in, low.slot_legs)
    own_low.wait()
    for h in range(2):
        low.send_hop("a1", h)
    for h in range(2):
        low.spread("own", h)
    own_mid.wait()
    transfer(
        w_mid.at[mid_rows], ws_mid.at[0, mid_rows, theirs, :], mid_first, (0,), mate
    ).wait_recv()
    mid.send_hop("a1", 0)
    mix_left(low, "own")

    own_top.wait()
    for n, (_, part, peer) in enumerate(quarters):
        transfer(
            w_top.at[rows_at(top.own_at, 64)], top_parts.at[part], top_first, (n,), peer
        ).wait_recv()

    @pl.loop(0, 4)
    def _(n):
        for part in range(4):
            half_in[pl.ds(0, 16), part * 4 : part * 4 + 4, :] = top_parts[
                part, pl.ds(n * 16, 16), :, :
            ].astype(F32)
        ws_top[0, rows_at(top.own_at + n * 16, 16), :, :] = half_in[pl.ds(0, 16)].astype(BF)

    for h in range(2):
        low.recv_hop("a1", h)
        low.send_hop("relay", h)
        low.send_hop("own", h)
        low.spread("first", h)
    mid.recv_hop("a1", 0)
    mid.send_hop("relay", 0)
    mid.send_hop("own", 0)
    for name in ("own", "first"):
        mid.spread(name, 0)
        mid.share(name, 0, mid.own_at, 128, mate)
    for h in range(2):
        low.relay("own", h)
    mix_left(low, "first")
    for h in range(2):
        low.relay("first", h)
    for h in range(2):
        low.recv_hop("relay", h)
        low.spread("both", h)
        low.recv_hop("own", h)
        low.spread("second", h)
    top.send_hop("a1", 0)
    mid.relay("own", 0)
    mid.relay("first", 0)
    mix_left(low, "both")
    for h in range(2):
        low.relay("both", h)
    mix_left(low, "second")
    for h in range(2):
        low.relay("second", h)
    mid.recv_hop("relay", 0)
    mid.spread("both", 0)
    mid.share("both", 0, mid.own_at, 128, mate)
    mid.recv_hop("own", 0)
    mid.spread("second", 0)
    mid.share("second", 0, mid.own_at, 128, mate)
    top.recv_hop("a1", 0)
    top.send_hop("relay", 0)
    top.send_hop("own", 0)
    for name in ("own", "first"):
        top.spread(name, 0)
        top.share(name, 0, top.own_at, 64, across)
    for name in ("own", "first", "both", "second"):
        for h in range(2):
            low.arrive(name, h)
    low.finish_local()
    contract(low)

    sums[...] = acc[...].astype(BF)
    ring_start(lambda one: sums.at[:, rows_at(one * 16, 16), :], lambda d: inbox.at[d], rs_sem)
    mid.relay("both", 0)
    mid.relay("second", 0)
    ring_recv(lambda d: inbox.at[d], rs_sem)
    total = acc[:, rows_at(leg * 16, 16), :]
    for d in range(1, LEGS):
        total = total + inbox[d].astype(F32)
    block[...] = total.astype(BF)
    ops_a[core, :, rows_at(leg * 16, 16), :] = total.astype(BF)
    ring_start(
        lambda one: block, lambda d: ops_a.at[core, :, rows_at(leg * 16, 16), :], ag_sem
    )
    top.recv_hop("relay", 0)
    top.spread("both", 0)
    top.share("both", 0, top.own_at, 64, across)
    ring_recv(
        lambda d: ops_a.at[core, :, rows_at((leg - d + LEGS) % LEGS * 16, 16), :], ag_sem
    )
    op_send = transfer(ops_a.at[core], ops_a.at[core], op_sem, (0,), mate)
    op_send.start()
    top.recv_hop("own", 0)
    top.spread("second", 0)
    top.share("second", 0, top.own_at, 64, across)
    top.relay("own", 0)
    top.relay("first", 0)
    transfer(ops_a.at[1 - core], ops_a.at[1 - core], op_sem, (0,), mate).wait_recv()

    load_left(ops_a.at[0], mid.n_left, mid.left_at)
    for t in range(2):
        right_t[t] = ops_a[1, t].T
    load_right(right_t, mid.slot_legs)
    for name in ("own", "first", "both", "second"):
        mid.shared(name, 0, 128 - core * 128, 128, mate)
        mix_left(mid, name)
        top.shared(name, 0, core * 128 + (1 - side) * 64, 64, across)
        top.share(name, 1, core * 128, 128, mate)
        if name in ("both", "second"):
            top.relay(name, 0)
    for name in ("own", "first", "both", "second"):
        mid.arrive(name, 0)
    mid.finish_local()
    contract(mid)

    ring_sent(lambda one: sums.at[:, rows_at(one * 16, 16), :], rs_sem)
    sums[...] = acc[...].astype(BF)
    mate_send = transfer(sums.at[1 - core], mate_in, mate_sem, (0,), mate)
    mate_send.start()
    transfer(mate_in, mate_in, mate_sem, (0,), mate).wait_recv()
    mid_sum[...] = (acc[core] + mate_in[...].astype(F32)).astype(BF)
    ring_start(lambda one: mid_sum.at[rows_at(one * 16, 16), :], lambda d: mid_in.at[d], rs2_sem)
    own_rows = rows_at(leg * 16, 16)
    total = acc[core, own_rows, :] + mate_in[own_rows, :].astype(F32)
    ring_recv(lambda d: mid_in.at[d], rs2_sem)
    for d in range(1, LEGS):
        total = total + mid_in[d].astype(F32)
    mid_block[...] = total.astype(BF)
    ops_b[side, core, own_rows, :] = total.astype(BF)
    ring_start(lambda one: mid_block, lambda d: ops_b.at[side, core, own_rows, :], ag2_sem)
    ring_recv(
        lambda d: ops_b.at[side, core, rows_at((leg - d + LEGS) % LEGS * 16, 16), :], ag2_sem
    )
    ours = ops_b.at[side, core]
    op2_sends = [
        transfer(ours, ours, op2_sem, (0,), mate),
        transfer(ours, ours, op2_sem, (1,), across),
    ]
    for copy in op2_sends:
        copy.start()
    other = ops_b.at[1 - side, core]
    transfer(other, other, op2_sem, (1,), across).wait_recv()
    op2_sends.append(transfer(other, other, op2_sem, (2,), mate))
    op2_sends[-1].start()
    for n, ref in ((0, ops_b.at[side, 1 - core]), (2, ops_b.at[1 - side, 1 - core])):
        transfer(ref, ref, op2_sem, (n,), mate).wait_recv()

    load_left(ops_b.at[0], top.n_left, top.left_at)
    for t in range(2):
        right_t[t] = ops_b[1, t].T
    load_right(right_t, top.slot_legs)
    for name in ("own", "first", "both", "second"):
        top.shared(name, 1, 128 - core * 128, 128, mate)
        mix_left(top, name)
    for name in ("own", "first", "both", "second"):
        top.arrive(name, 0)
    top.finish_local()
    contract(top)

    half_sends = []
    for n in range(2):
        copy = transfer(
            acc.at[:, rows_at((2 * n + 1 - core) * 64, 64), :],
            quarter_in.at[n],
            half_sem, (n,), mate,
        )
        copy.start()
        half_sends.append(copy)
    for n in range(2):
        transfer(quarter_in.at[n], quarter_in.at[n], half_sem, (n,), mate).wait_recv()
        half_sum[n] = acc[:, rows_at((2 * n + core) * 64, 64), :] + quarter_in[n]
    side_send = transfer(half_sum.at[1 - side], quarter_in.at[2], quarter_sem, (0,), across)
    side_send.start()
    transfer(quarter_in.at[2], quarter_in.at[2], quarter_sem, (0,), across).wait_recv()
    for t in range(2):
        part = half_sum[side, t] + quarter_in[2, t]
        for one in range(LEGS):
            rows_out[one, t * 4 : t * 4 + 4, :] = part[one * 4 : one * 4 + 4]
    ring_start(lambda one: rows_out.at[one], lambda d: rows_in.at[d], rs3_sem)
    total = rows_out[leg]
    ring_recv(lambda d: rows_in.at[d], rs3_sem)
    for d in range(1, LEGS):
        total = total + rows_in[d]
    for t in range(2):
        out[0, t] = total[t * 4 : t * 4 + 4]

    for level in (low, mid, top):
        level.finish()
    mid_out.wait_send()
    for copy in (*top_sends, op_send, mate_send, *op2_sends, *half_sends, side_send):
        copy.wait_send()
    ring_sent(lambda one: block, ag_sem)
    ring_sent(lambda one: mid_sum.at[rows_at(one * 16, 16), :], rs2_sem)
    ring_sent(lambda one: mid_block, ag2_sem)
    ring_sent(lambda one: rows_out.at[one], rs3_sem)


def on_device(tensor_low, tensor_mid, tensor_top, child_operators, term_choice):
    bank, choice = child_operators[0], term_choice[0]

    def chosen(side):
        return jnp.stack(
            [
                lax.dynamic_index_in_dim(bank[side], choice[t, side], 0, keepdims=False)
                for t in range(2)
            ]
        )

    left, right = chosen(0), jnp.swapaxes(chosen(1), 1, 2)
    dma, vmem = pltpu.SemaphoreType.DMA, pltpu.VMEM

    def level_sems(halves):
        return [
            dma((2, 3, halves)),
            dma((2, 4, halves)),
            dma((2, 4, halves)),
            dma((2, 4, halves)),
            dma((4, halves)),
            dma((2, 2, 4)),
        ]

    hbm = pl.BlockSpec(memory_space=pl.ANY)
    inside = pl.BlockSpec(memory_space=pltpu.VMEM)
    return pl.pallas_call(
        kernel,
        out_shape=jax.ShapeDtypeStruct((1, 2, 4, BOND), F32),
        in_specs=[hbm, hbm, hbm, inside, inside],
        out_specs=inside,
        scratch_shapes=[
            vmem((4, 256, 16, BOND), BF),
            vmem((4, 256, 16, BOND), BF),
            vmem((4, 256, 16, BOND), BF),
            vmem((64, 256, BOND), BF),
            vmem((32, 256, BOND), BF),
            vmem((16, 256, BOND), BF),
            vmem((4, 64, 4, BOND), BF),
            vmem((4096, 128), F32),
            vmem((4096, 128), F32),
            vmem((8192, 128), F32),
            vmem((8192, 128), F32),
            vmem((2, 256, BOND), BF),
            vmem((2, BOND, BOND), F32),
            vmem((128, BOND), BF),
            vmem((128, BOND), BF),
            vmem((2, BOND, BOND), BF),
            vmem((2, BOND, BOND), BF),
            vmem((LEGS, 2, 16, BOND), BF),
            vmem((2, 16, BOND), BF),
            vmem((2, 2, BOND, BOND), BF),
            vmem((BOND, BOND), BF),
            vmem((BOND, BOND), BF),
            vmem((LEGS, 16, BOND), BF),
            vmem((16, BOND), BF),
            vmem((2, 2, BOND, BOND), BF),
            *level_sems(2),
            *level_sems(1),
            *level_sems(1),
            dma((3,)),
            dma((2, 1)),
            dma((2, 3)),
            dma((2, LEGS)),
            dma((2, LEGS)),
            dma((2, 1)),
            dma((2, 1)),
            dma((2, LEGS)),
            dma((2, LEGS)),
            dma((2, 3)),
            dma((2, 2)),
            dma((2, 1)),
            dma((2, LEGS)),
            vmem((16, 16, BOND), F32),
            vmem((2, 2, 64, BOND), F32),
            vmem((3, 2, 64, BOND), F32),
            vmem((LEGS, 8, BOND), F32),
            vmem((LEGS, 8, BOND), F32),
        ],
        compiler_params=pltpu.CompilerParams(
            collective_id=0, has_side_effects=True, vmem_limit_bytes=67043328
        ),
    )(tensor_low[0], tensor_mid[0], tensor_top[0], left, right)


def solution(mesh):
    return jax.shard_map(
        on_device,
        mesh=mesh,
        in_specs=(
            P("leaf", None, "leg", None),
            P("leaf", None, "leg", None),
            P("leaf", None, "leg", None),
            P("leaf", None, None, None, None),
            P("leaf", None, None),
        ),
        out_specs=P("leaf", None, "leg", None),
        check_vma=False,
    )
```

time: 325 us -> 240 us (0.74)
  Pallas kernels: 0 us -> 225 us
  waiting for transfers between devices: 163 us -> 0 us
  starting transfers between devices: 82.9 us -> 0 us
  local copies, waits for them, and re-layouts: 29.2 us -> 4.25 us
  blocking collectives: 22.9 us -> 0 us
  matrix products: 11.8 us -> 0 us
  other arithmetic: 5.35 us -> 1.43 us
    pallas_call x0 -> x1, Pallas kernels: none -> 225 us  [on_device(): pl.pallas_call(kernel, out_shape=jax.ShapeDtypeStruct((1, 2, 4, BOND), F3...]
    all_to_all x10 -> x0, waiting for transfers between devices: 139 us -> none  [the longest x6 112 us: regroup(): lax.all_to_all(flattened, 'leg', split_axis=1, concat_axis=3, tiled=True)]
    all_to_all x10 -> x0, starting transfers between devices: 46.4 us -> none  [the longest x6 30.2 us: regroup(): lax.all_to_all(flattened, 'leg', split_axis=1, concat_axis=3, tiled=True)]
    ppermute x8 -> x0, starting transfers between devices: 36.5 us -> none  [from_partner(): return lax.ppermute(block, axis, route)]
    ppermute x8 -> x0, waiting for transfers between devices: 24.5 us -> none  [from_partner(): return lax.ppermute(block, axis, route)]
    all_to_all x2 -> x0, blocking collectives: 22.9 us -> none  [the longest x1 11.7 us: sent_and_summed(): lax.all_to_all(pieces, axis, split_axis=0, concat_axis=0, tiled=True)]
    dot_general x9 -> x0, matrix products: 11.8 us -> none  [the longest x3 5.06 us: renormalize_level(): jnp.einsum('tkas,ksb->tab', rotated_tensor, shifted_tensor, preferred_ele...]
    another operation x3 -> x0, local copies, waits for them, and re-layouts: 9.51 us -> none  [regroup(): shaped.reshape(stacked_count, leg_count, slice_width, group_size * row_co...]
  transfers between devices with their start and end apart: 18 -> 0, of which waited for: 16 -> 0; matrix products, arithmetic and copies ran while one was open for 13% -> 0% of each run, Pallas kernels for 0% -> 0%
where the time goes in v1:
time: 240 us; the launch traced here: 238 us
  Pallas kernels  225 us (94%)
  between operations  7.34 us (3%)
  local copies, waits for them, and re-layouts  4.25 us (2%)
    pallas_call x1, Pallas kernels, on_device(): pl.pallas_call(kernel, out_shape=jax.ShapeDtypeStruct((1, 2, 4, BOND), F3...  225 us

profile of v1, /device:TPU:1, one launch (start us, length us, event | category | flops | bytes accessed | tf_op | source)
XLA Modules:
  0.0 238.3 jit_solution(13404572647306865632)
XLA Ops:
  0.0 1.4 fusion.1
  8.7 1.3 fusion
  10.1 0.1 copy.6
  10.2 0.1 copy.7
  10.3 0.7 maximum_bitcast_fusion.right_in
  11.0 0.7 pad_maximum_fusion.left_in
  11.7 225.3 %shard_map.55 = f32[1,2,4,256]{3,2,1,0:T(4,128)} custom-call(bf16[256,16,256]{2,1,0:T(8,128)(2,1)} %bitcast.16, bf16[256,8,256]{2,1,0:T(8,128)(2,1)} %bitcast.17, bf16[256,4,256]{2,1,0:T(4,128)(2,1)} %bitcast.20, bf16[2,256,256]{2,1,0:T(8,128)(2,1)} %pad_maximum_fusion.left_in, bf16[2,256,256]{2,1,0:T(8,128)(2,1)} %maximum_bitcast_fusion.right_in), custom_call_target="tpu_custom_call" | custom-call | tf_op jit(solution)/shard_map/pallas_call | solution.py:529
  237.0 1.3 copy.9
  (2 shorter events, 0.0 us)

commit v2 on v1

--- a/solution.py
+++ b/solution.py
@@ -157,15 +157,16 @@
 
 
 def kernel(
-    w_low, w_mid, w_top, left_in, right_in, out,
-    ws_low, ws_mid, ws_top, wl_low, wl_mid, wl_top, top_parts, flat_0, flat_1, ys_0, ys_1, zs, acc, l_cat, r_cat,
-    right_t, sums, inbox, block, ops_a, mate_in, mid_sum, mid_in, mid_block, ops_b,
+    w_low, w_mid, w_top, bank_in, choice, out,
+    ws_low, ws_mid, ws_top, wl_low, wl_mid, wl_top, top_parts, by_row_low, by_row_mid, ys_0, ys_1,
+    zs, acc, l_cat, r_cat, right_t, bank, sums, inbox, block, ops_a, mate_in, mid_sum, mid_in,
+    mid_block, ops_b,
     low_a, low_b1, low_bd, low_br, low_loc, low_share,
     mid_a, mid_b1, mid_bd, mid_br, mid_loc, mid_share,
     top_a, top_b1, top_bd, top_br, top_loc, top_share,
     first_sem, mid_first, top_first, rs_sem, ag_sem, op_sem,
     mate_sem, rs2_sem, ag2_sem, op2_sem, half_sem, quarter_sem, rs3_sem,
-    half_in, half_sum, quarter_in, rows_out, rows_in,
+    wide, half_sum, half_in, side_sum, side_in, rows_out, rows_in,
 ):
     leaf, leg = lax.axis_index("leaf"), lax.axis_index("leg")
     core, z = leaf % 2, leaf // 2
@@ -177,6 +178,39 @@
     across = (leaf + 2 - 4 * side, leg)
     cross = (leaf + 2 - 4 * side + 1 - 2 * core, leg)
     env = {"leaf": leaf, "leg": leg, "core": core}
+    near, far = (x_near, y_near), (x_far, y_far)
+
+    low = Level(
+        env, ws_low, wl_low, (low_a, low_b1, low_bd, low_br, low_loc, low_share),
+        256, 0, near_x + 2 * near_y, near, far, 2,
+    )
+    mid = Level(
+        env, ws_mid, wl_mid, (mid_a, mid_b1, mid_bd, mid_br, mid_loc, mid_share),
+        128, core * 128, near_x + 2 * near_y, near, far, 1,
+    )
+    top = Level(
+        env, ws_top, wl_top, (top_a, top_b1, top_bd, top_br, top_loc, top_share),
+        64, core * 128 + side * 64, far_x + 2 * far_y, far, near, 1,
+    )
+    q = side * 2 + core
+    mine, theirs = rows_at(core * 8, 8), rows_at(8 - core * 8, 8)
+    mid_rows, mate_rows = rows_at(core * 128, 128), rows_at(128 - core * 128, 128)
+
+    own_low = [
+        pltpu.make_async_copy(
+            w_low.at[:, pl.ds(h * 8, 8), :], ws_low.at[0, :, pl.ds(h * 8, 8), :], first_sem.at[h]
+        )
+        for h in range(2)
+    ]
+    own_mid = pltpu.make_async_copy(
+        w_mid.at[mid_rows], ws_mid.at[0, mid_rows, mine, :], first_sem.at[2]
+    )
+    own_top = pltpu.make_async_copy(
+        w_top.at[rows_at(top.own_at, 64)], top_parts.at[q], first_sem.at[3]
+    )
+    own_bank = pltpu.make_async_copy(bank_in, bank, first_sem.at[4])
+    for copy in (*own_low, own_bank, own_mid, own_top):
+        copy.start()
 
     barrier = pltpu.get_barrier_semaphore()
 
@@ -188,33 +222,13 @@
         pl.semaphore_signal(barrier, inc=1, device_id=peer, device_id_type=MESH)
     pl.semaphore_wait(barrier, LEGS + 2)
 
-    low = Level(
-        env, ws_low, wl_low, (low_a, low_b1, low_bd, low_br, low_loc, low_share),
-        256, 0, near_x + 2 * near_y, (x_near, y_near), (x_far, y_far), 2,
-    )
-    mid = Level(
-        env, ws_mid, wl_mid, (mid_a, mid_b1, mid_bd, mid_br, mid_loc, mid_share),
-        128, core * 128, far_x + 2 * far_y, (x_far, y_far), (x_near, y_near), 1,
-    )
-    top = Level(
-        env, ws_top, wl_top, (top_a, top_b1, top_bd, top_br, top_loc, top_share),
-        64, core * 128 + side * 64, near_x + 2 * near_y, (x_near, y_near), (x_far, y_far), 1,
-    )
-
-    own_low = pltpu.make_async_copy(w_low, ws_low.at[0], first_sem.at[0])
-    own_low.start()
-    mine = pl.ds(pl.multiple_of(core * 8, 8), 8)
-    theirs = pl.ds(pl.multiple_of(8 - core * 8, 8), 8)
-    mid_rows, mate_rows = rows_at(core * 128, 128), rows_at(128 - core * 128, 128)
+    for h in range(2):
+        own_low[h].wait()
+        low.send_hop("a1", h)
     mid_out = transfer(
         w_mid.at[mate_rows], ws_mid.at[0, mate_rows, mine, :], mid_first, (0,), mate
     )
     mid_out.start()
-    own_mid = pltpu.make_async_copy(
-        w_mid.at[mid_rows], ws_mid.at[0, mid_rows, mine, :], first_sem.at[1]
-    )
-    own_mid.start()
-    q = side * 2 + core
     quarters = [
         ((1 - core) * 128 + side * 64, side * 2 + 1 - core, mate),
         (core * 128 + (1 - side) * 64, (1 - side) * 2 + core, across),
@@ -225,58 +239,81 @@
         copy = transfer(w_top.at[rows_at(start, 64)], top_parts.at[q], top_first, (n,), peer)
         copy.start()
         top_sends.append(copy)
-    own_top = pltpu.make_async_copy(
-        w_top.at[rows_at(top.own_at, 64)], top_parts.at[q], first_sem.at[2]
-    )
-    own_top.start()
-
-    def load_left(ref, n_left, at):
+    for h in range(2):
+        low.spread("own", h)
+
+    def load_left(read, n_left, at):
         for t in range(2):
-            l_cat[t * n_left : (t + 1) * n_left] = ref[t, rows_at(at, n_left), :]
-
-    def load_right(ref, legs):
+            l_cat[t * n_left : (t + 1) * n_left] = read(t, rows_at(at, n_left))
+
+    def load_right(legs):
         for t in range(2):
             for slot, one in enumerate(legs):
                 start = t * 64 + slot * 16
-                r_cat[start : start + 16] = ref[t, rows_at(one * 16, 16), :]
-
-    def mix_left(level, name):
-        slot, n_left = level.slot_of[name], level.n_left
-
-        @pl.loop(0, 16)
+                r_cat[start : start + 16] = right_t[t, rows_at(one * 16, 16), :]
+
+    def mix_rows(slot, s, rows, n_left):
+        mixed = jnp.dot(l_cat[: 2 * n_left], rows, preferred_element_type=F32)
+        span = pl.ds(slot * 16 + s, 2 * n_left, stride=64)
+        ys_0[span, :] = mixed[:, :128]
+        ys_1[span, :] = mixed[:, 128:]
+
+    def mix_low(name):
+        slot = low.slot_of[name]
+
+        @pl.loop(0, 16, unroll=2)
         def _(n):
-            rows = level.ws[slot, pl.ds(n * 16, 16), :, :]
-            rows = rows.reshape(256, BOND).astype(F32)
-            for n_col, ref in enumerate((flat_0, flat_1)):
-                ref[pl.ds(n * 256, 256), :] = rows[:, n_col * 128 : n_col * 128 + 128]
-
-        left = l_cat[: 2 * n_left]
-
-        @pl.loop(0, 16)
+            by_row_low[:, pl.ds(n * 16, 16), :] = jnp.swapaxes(ws_low[slot, pl.ds(n * 16, 16)], 0, 1)
+
+        @pl.loop(0, 16, unroll=4)
         def _(s):
-            for source, target in ((flat_0, ys_0), (flat_1, ys_1)):
-                rows = source[pl.ds(s, 256, stride=16), :].astype(BF)
-                target[pl.ds(slot * 16 + s, 2 * n_left, stride=64), :] = jnp.dot(
-                    left, rows, preferred_element_type=F32
-                )
+            mix_rows(slot, s, by_row_low[s], low.n_left)
+
+    def turn_mid(name, half):
+        slot = mid.slot_of[name]
+
+        @pl.loop(0, 8, unroll=2)
+        def _(n):
+            rows = rows_at(half * 128 + n * 16, 16)
+            by_row_mid[pl.ds(slot * 16, 16), rows, :] = jnp.swapaxes(ws_mid[slot, rows], 0, 1)
+
+    def mix_mid():
+        @pl.loop(0, 64, unroll=8)
+        def _(s):
+            mix_rows(0, s, by_row_mid[s], mid.n_left)
+
+    def turn_top(name):
+        slot = top.slot_of[name]
+
+        @pl.loop(0, 16, unroll=2)
+        def _(n):
+            turned = jnp.swapaxes(ws_top[slot, pl.ds(n * 16, 16)], 0, 1)
+            for s in range(16):
+                ws_low[slot, s * 16 + n] = turned[s]
+
+    def mix_top():
+        @pl.loop(0, 64, unroll=8)
+        def _(s):
+            rows = ws_low[s // 16, pl.ds(s % 16 * 16, 16)]
+            mix_rows(0, s, rows.reshape(256, BOND), top.n_left)
 
     def contract(level):
         acc[...] = jnp.zeros_like(acc)
         n_left = level.n_left
 
-        @pl.loop(0, n_left // 4)
+        @pl.loop(0, n_left // 4, unroll=2)
         def _(n):
             for k in range(4):
                 turned = jnp.dot(
                     r_cat[...], level.wl[n * 4 + k], preferred_element_type=F32
                 ).astype(BF)
                 for t in range(2):
-                    zs[t, k * 64 : (k + 1) * 64] = turned[t * 64 : (t + 1) * 64]
+                    zs[n % 2, t, k * 64 : (k + 1) * 64] = turned[t * 64 : (t + 1) * 64]
             for t in range(2):
                 span = rows_at((t * n_left + n * 4) * 64, 256)
                 rows = jnp.concatenate([ys_0[span, :], ys_1[span, :]], axis=1).astype(BF)
                 acc[t] += lax.dot_general(
-                    zs[t], rows, (((0,), (0,)), ((), ())), preferred_element_type=F32
+                    zs[n % 2, t], rows, (((0,), (0,)), ((), ())), preferred_element_type=F32
                 )
 
     def ring_start(src_of, dst_of, sem):
@@ -298,19 +335,15 @@
             ref = src_of(one)
             transfer(ref, ref, sem, (d,), (leaf, one)).wait_send()
 
-    load_left(left_in, low.n_left, low.left_at)
-    load_right(right_in, low.slot_legs)
-    own_low.wait()
-    for h in range(2):
-        low.send_hop("a1", h)
-    for h in range(2):
-        low.spread("own", h)
-    own_mid.wait()
-    transfer(
-        w_mid.at[mid_rows], ws_mid.at[0, mid_rows, theirs, :], mid_first, (0,), mate
-    ).wait_recv()
-    mid.send_hop("a1", 0)
-    mix_left(low, "own")
+    def mid_share(name):
+        mid.share(name, 0, mid.own_at, 128, mate)
+
+    def mid_shared(name):
+        mid.shared(name, 0, 128 - core * 128, 128, mate)
+
+    def top_across(name):
+        top.shared(name, 0, core * 128 + (1 - side) * 64, 64, across)
+        top.share(name, 1, core * 128, 128, mate)
 
     own_top.wait()
     for n, (_, part, peer) in enumerate(quarters):
@@ -321,53 +354,63 @@
     @pl.loop(0, 4)
     def _(n):
         for part in range(4):
-            half_in[pl.ds(0, 16), part * 4 : part * 4 + 4, :] = top_parts[
-                part, pl.ds(n * 16, 16), :, :
-            ].astype(F32)
-        ws_top[0, rows_at(top.own_at + n * 16, 16), :, :] = half_in[pl.ds(0, 16)].astype(BF)
+            wide[:, part * 4 : part * 4 + 4, :] = top_parts[part, pl.ds(n * 16, 16), :, :].astype(
+                F32
+            )
+        ws_top[0, rows_at(top.own_at + n * 16, 16), :, :] = wide[:, :16, :].astype(BF)
+
+    own_bank.wait()
+    load_left(lambda t, rows: bank[0, choice[t, 0], rows, :], low.n_left, low.left_at)
+    for t in range(2):
+        right_t[t] = bank[1, choice[t, 1]].T
+    load_right(low.slot_legs)
+    top.send_hop("a1", 0)
+    own_mid.wait()
+    transfer(
+        w_mid.at[mid_rows], ws_mid.at[0, mid_rows, theirs, :], mid_first, (0,), mate
+    ).wait_recv()
+    mid_share("own")
+    top.share("own", 0, top.own_at, 64, across)
+    mix_low("own")
 
     for h in range(2):
         low.recv_hop("a1", h)
         low.send_hop("relay", h)
         low.send_hop("own", h)
         low.spread("first", h)
-    mid.recv_hop("a1", 0)
-    mid.send_hop("relay", 0)
-    mid.send_hop("own", 0)
-    for name in ("own", "first"):
-        mid.spread(name, 0)
-        mid.share(name, 0, mid.own_at, 128, mate)
-    for h in range(2):
-        low.relay("own", h)
-    mix_left(low, "first")
-    for h in range(2):
-        low.relay("first", h)
+        if h == 0:
+            for n in range(2):
+                low.relay("own", n)
+    low.relay("first", 0)
+    mix_low("first")
+    low.relay("first", 1)
+    turn_mid("own", core)
+    mid_shared("own")
+    turn_mid("own", 1 - core)
+    mid.spread("own", 0)
     for h in range(2):
         low.recv_hop("relay", h)
         low.spread("both", h)
         low.recv_hop("own", h)
         low.spread("second", h)
-    top.send_hop("a1", 0)
-    mid.relay("own", 0)
-    mid.relay("first", 0)
-    mix_left(low, "both")
-    for h in range(2):
-        low.relay("both", h)
-    mix_left(low, "second")
-    for h in range(2):
-        low.relay("second", h)
-    mid.recv_hop("relay", 0)
-    mid.spread("both", 0)
-    mid.share("both", 0, mid.own_at, 128, mate)
-    mid.recv_hop("own", 0)
-    mid.spread("second", 0)
-    mid.share("second", 0, mid.own_at, 128, mate)
+        if h == 0:
+            low.relay("both", 0)
+            low.relay("second", 0)
+    mid.send_hop("a1", 0)
+    low.relay("both", 1)
+    mix_low("both")
+    low.relay("second", 1)
     top.recv_hop("a1", 0)
     top.send_hop("relay", 0)
     top.send_hop("own", 0)
-    for name in ("own", "first"):
-        top.spread(name, 0)
-        top.share(name, 0, top.own_at, 64, across)
+    top.share("first", 0, top.own_at, 64, across)
+    mix_low("second")
+    mid.relay("own", 0)
+    mid.recv_hop("a1", 0)
+    mid.send_hop("relay", 0)
+    mid.send_hop("own", 0)
+    mid.spread("first", 0)
+    mid_share("first")
     for name in ("own", "first", "both", "second"):
         for h in range(2):
             low.arrive(name, h)
@@ -376,8 +419,13 @@
 
     sums[...] = acc[...].astype(BF)
     ring_start(lambda one: sums.at[:, rows_at(one * 16, 16), :], lambda d: inbox.at[d], rs_sem)
-    mid.relay("both", 0)
-    mid.relay("second", 0)
+    turn_mid("first", core)
+    mid_shared("second")
+    turn_mid("second", 1 - core)
+    mid.recv_hop("relay", 0)
+    mid.spread("both", 0)
+    mid_share("both")
+    mid.relay("first", 0)
     ring_recv(lambda d: inbox.at[d], rs_sem)
     total = acc[:, rows_at(leg * 16, 16), :]
     for d in range(1, LEGS):
@@ -387,32 +435,36 @@
     ring_start(
         lambda one: block, lambda d: ops_a.at[core, :, rows_at(leg * 16, 16), :], ag_sem
     )
-    top.recv_hop("relay", 0)
-    top.spread("both", 0)
-    top.share("both", 0, top.own_at, 64, across)
+    mid.recv_hop("own", 0)
+    mid.spread("second", 0)
+    mid_share("second")
+    turn_mid("both", core)
+    turn_mid("second", core)
     ring_recv(
         lambda d: ops_a.at[core, :, rows_at((leg - d + LEGS) % LEGS * 16, 16), :], ag_sem
     )
     op_send = transfer(ops_a.at[core], ops_a.at[core], op_sem, (0,), mate)
     op_send.start()
+    mid.relay("both", 0)
+    top.recv_hop("relay", 0)
+    top.share("both", 0, top.own_at, 64, across)
     top.recv_hop("own", 0)
-    top.spread("second", 0)
     top.share("second", 0, top.own_at, 64, across)
-    top.relay("own", 0)
-    top.relay("first", 0)
+    for name in ("own", "first", "both", "second"):
+        top.spread(name, 0)
+    mid_shared("both")
+    turn_mid("both", 1 - core)
+    mid_shared("first")
+    turn_mid("first", 1 - core)
+    mid.relay("second", 0)
+    low.finish()
     transfer(ops_a.at[1 - core], ops_a.at[1 - core], op_sem, (0,), mate).wait_recv()
 
-    load_left(ops_a.at[0], mid.n_left, mid.left_at)
+    load_left(lambda t, rows: ops_a[0, t, rows, :], mid.n_left, mid.left_at)
     for t in range(2):
         right_t[t] = ops_a[1, t].T
-    load_right(right_t, mid.slot_legs)
-    for name in ("own", "first", "both", "second"):
-        mid.shared(name, 0, 128 - core * 128, 128, mate)
-        mix_left(mid, name)
-        top.shared(name, 0, core * 128 + (1 - side) * 64, 64, across)
-        top.share(name, 1, core * 128, 128, mate)
-        if name in ("both", "second"):
-            top.relay(name, 0)
+    load_right(mid.slot_legs)
+    mix_mid()
     for name in ("own", "first", "both", "second"):
         mid.arrive(name, 0)
     mid.finish_local()
@@ -422,17 +474,23 @@
     sums[...] = acc[...].astype(BF)
     mate_send = transfer(sums.at[1 - core], mate_in, mate_sem, (0,), mate)
     mate_send.start()
+    top_across("own")
+    top_across("first")
     transfer(mate_in, mate_in, mate_sem, (0,), mate).wait_recv()
     mid_sum[...] = (acc[core] + mate_in[...].astype(F32)).astype(BF)
     ring_start(lambda one: mid_sum.at[rows_at(one * 16, 16), :], lambda d: mid_in.at[d], rs2_sem)
     own_rows = rows_at(leg * 16, 16)
     total = acc[core, own_rows, :] + mate_in[own_rows, :].astype(F32)
+    top.shared("own", 1, 128 - core * 128, 128, mate)
+    turn_top("own")
+    top_across("both")
     ring_recv(lambda d: mid_in.at[d], rs2_sem)
     for d in range(1, LEGS):
         total = total + mid_in[d].astype(F32)
     mid_block[...] = total.astype(BF)
     ops_b[side, core, own_rows, :] = total.astype(BF)
     ring_start(lambda one: mid_block, lambda d: ops_b.at[side, core, own_rows, :], ag2_sem)
+    top_across("second")
     ring_recv(
         lambda d: ops_b.at[side, core, rows_at((leg - d + LEGS) % LEGS * 16, 16), :], ag2_sem
     )
@@ -443,53 +501,61 @@
     ]
     for copy in op2_sends:
         copy.start()
+    top.shared("both", 1, 128 - core * 128, 128, mate)
+    turn_top("both")
+    top.relay("own", 0)
+    top.relay("first", 0)
+    top.relay("both", 0)
     other = ops_b.at[1 - side, core]
     transfer(other, other, op2_sem, (1,), across).wait_recv()
     op2_sends.append(transfer(other, other, op2_sem, (2,), mate))
     op2_sends[-1].start()
+    top.relay("second", 0)
+    for name in ("first", "second"):
+        top.shared(name, 1, 128 - core * 128, 128, mate)
+        turn_top(name)
     for n, ref in ((0, ops_b.at[side, 1 - core]), (2, ops_b.at[1 - side, 1 - core])):
         transfer(ref, ref, op2_sem, (n,), mate).wait_recv()
 
-    load_left(ops_b.at[0], top.n_left, top.left_at)
+    load_left(lambda t, rows: ops_b[0, t, rows, :], top.n_left, top.left_at)
     for t in range(2):
         right_t[t] = ops_b[1, t].T
-    load_right(right_t, top.slot_legs)
-    for name in ("own", "first", "both", "second"):
-        top.shared(name, 1, 128 - core * 128, 128, mate)
-        mix_left(top, name)
+    load_right(top.slot_legs)
+    mix_top()
     for name in ("own", "first", "both", "second"):
         top.arrive(name, 0)
     top.finish_local()
     contract(top)
 
+    for one in range(LEGS):
+        for t in range(2):
+            for part in range(4):
+                at = part * 64 + one * 4
+                wide[one, part * 8 + t * 4 : part * 8 + t * 4 + 4, :] = acc[t, at : at + 4, :]
+    rows_out[...] = wide[...].astype(BF)
+    ring_start(lambda one: rows_out.at[one], lambda d: rows_in.at[d], rs3_sem)
+    total = wide[leg]
+    ring_recv(lambda d: rows_in.at[d], rs3_sem)
+    for d in range(1, LEGS):
+        total = total + rows_in[d].astype(F32)
+    half_sum[...] = total.reshape(2, 2, 8, BOND)
     half_sends = []
     for n in range(2):
-        copy = transfer(
-            acc.at[:, rows_at((2 * n + 1 - core) * 64, 64), :],
-            quarter_in.at[n],
-            half_sem, (n,), mate,
-        )
+        copy = transfer(half_sum.at[n, 1 - core], half_in.at[n], half_sem, (n,), mate)
         copy.start()
         half_sends.append(copy)
     for n in range(2):
-        transfer(quarter_in.at[n], quarter_in.at[n], half_sem, (n,), mate).wait_recv()
-        half_sum[n] = acc[:, rows_at((2 * n + core) * 64, 64), :] + quarter_in[n]
-    side_send = transfer(half_sum.at[1 - side], quarter_in.at[2], quarter_sem, (0,), across)
+        transfer(half_in.at[n], half_in.at[n], half_sem, (n,), mate).wait_recv()
+    side_sum[...] = half_sum[1 - side, core] + half_in[1 - side]
+    side_send = transfer(side_sum, side_in, quarter_sem, (0,), across)
     side_send.start()
-    transfer(quarter_in.at[2], quarter_in.at[2], quarter_sem, (0,), across).wait_recv()
-    for t in range(2):
-        part = half_sum[side, t] + quarter_in[2, t]
-        for one in range(LEGS):
-            rows_out[one, t * 4 : t * 4 + 4, :] = part[one * 4 : one * 4 + 4]
-    ring_start(lambda one: rows_out.at[one], lambda d: rows_in.at[d], rs3_sem)
-    total = rows_out[leg]
-    ring_recv(lambda d: rows_in.at[d], rs3_sem)
-    for d in range(1, LEGS):
-        total = total + rows_in[d]
+    total = half_sum[side, core] + half_in[side]
+    transfer(side_in, side_in, quarter_sem, (0,), across).wait_recv()
+    total = total + side_in[...]
     for t in range(2):
         out[0, t] = total[t * 4 : t * 4 + 4]
 
-    for level in (low, mid, top):
+    for level in (mid, top):
         level.finish()
     mid_out.wait_send()
     for copy in (*top_sends, op_send, mate_send, *op2_sends, *half_sends, side_send):
@@ -501,17 +567,6 @@
 
 
 def on_device(tensor_low, tensor_mid, tensor_top, child_operators, term_choice):
-    bank, choice = child_operators[0], term_choice[0]
-
-    def chosen(side):
-        return jnp.stack(
-            [
-                lax.dynamic_index_in_dim(bank[side], choice[t, side], 0, keepdims=False)
-                for t in range(2)
-            ]
-        )
-
-    left, right = chosen(0), jnp.swapaxes(chosen(1), 1, 2)
     dma, vmem = pltpu.SemaphoreType.DMA, pltpu.VMEM
 
     def level_sems(halves):
@@ -529,7 +584,7 @@
     return pl.pallas_call(
         kernel,
         out_shape=jax.ShapeDtypeStruct((1, 2, 4, BOND), F32),
-        in_specs=[hbm, hbm, hbm, inside, inside],
+        in_specs=[hbm, hbm, hbm, hbm, pl.BlockSpec(memory_space=pltpu.SMEM)],
         out_specs=inside,
         scratch_shapes=[
             vmem((4, 256, 16, BOND), BF),
@@ -539,15 +594,16 @@
             vmem((32, 256, BOND), BF),
             vmem((16, 256, BOND), BF),
             vmem((4, 64, 4, BOND), BF),
-            vmem((4096, 128), F32),
-            vmem((4096, 128), F32),
+            vmem((16, 256, BOND), BF),
+            vmem((64, 256, BOND), BF),
             vmem((8192, 128), F32),
             vmem((8192, 128), F32),
-            vmem((2, 256, BOND), BF),
+            vmem((2, 2, 256, BOND), BF),
             vmem((2, BOND, BOND), F32),
             vmem((128, BOND), BF),
             vmem((128, BOND), BF),
             vmem((2, BOND, BOND), BF),
+            vmem((2, 4, BOND, BOND), BF),
             vmem((2, BOND, BOND), BF),
             vmem((LEGS, 2, 16, BOND), BF),
             vmem((2, 16, BOND), BF),
@@ -560,7 +616,7 @@
             *level_sems(2),
             *level_sems(1),
             *level_sems(1),
-            dma((3,)),
+            dma((5,)),
             dma((2, 1)),
             dma((2, 3)),
             dma((2, LEGS)),
@@ -573,16 +629,18 @@
             dma((2, 2)),
             dma((2, 1)),
             dma((2, LEGS)),
-            vmem((16, 16, BOND), F32),
-            vmem((2, 2, 64, BOND), F32),
-            vmem((3, 2, 64, BOND), F32),
-            vmem((LEGS, 8, BOND), F32),
-            vmem((LEGS, 8, BOND), F32),
+            vmem((LEGS, 32, BOND), F32),
+            vmem((2, 2, 8, BOND), F32),
+            vmem((2, 8, BOND), F32),
+            vmem((8, BOND), F32),
+            vmem((8, BOND), F32),
+            vmem((LEGS, 32, BOND), BF),
+            vmem((LEGS, 32, BOND), BF),
         ],
         compiler_params=pltpu.CompilerParams(
             collective_id=0, has_side_effects=True, vmem_limit_bytes=67043328
         ),
-    )(tensor_low[0], tensor_mid[0], tensor_top[0], left, right)
+    )(tensor_low[0], tensor_mid[0], tensor_top[0], child_operators[0], term_choice[0])
 
 
 def solution(mesh):

time: 240 us -> 178 us (0.74)
  Pallas kernels: 225 us -> 177 us
  between operations: 7.34 us -> 0.01 us
  local copies, waits for them, and re-layouts: 4.25 us -> 1.3 us
    pallas_call x1, Pallas kernels: 225 us -> 177 us  [on_device(): pl.pallas_call(kernel, out_shape=jax.ShapeDtypeStruct((1, 2, 4, BOND), F3...]
    slice x2 -> x0, local copies, waits for them, and re-layouts: 2.71 us -> none  [the longest x1 1.44 us: chosen(): choice[t, side]]
where the time goes in v2:
time: 178 us
  Pallas kernels  177 us (99%)
    pallas_call x1, Pallas kernels, on_device(): pl.pallas_call(kernel, out_shape=jax.ShapeDtypeStruct((1, 2, 4, BOND), F3...  177 us

profile of v2, /device:TPU:1, one launch (start us, length us, event | category | flops | bytes accessed | tf_op | source)
XLA Modules:
  0.0 177.8 jit_solution(17467528083421993435)
XLA Ops:
  0.0 176.5 %shard_map.55 = f32[1,2,4,256]{3,2,1,0:T(4,128)} custom-call(bf16[256,16,256]{2,1,0:T(8,128)(2,1)} %bitcast.5, bf16[256,8,256]{2,1,0:T(8,128)(2,1)} %bitcast.6, bf16[256,4,256]{2,1,0:T(4,128)(2,1)} %bitcast.8, bf16[2,4,256,256]{3,2,1,0:T(8,128)(2,1)} %bitcast.7, s32[2,2]{1,0:T(2,128)} %bitcast.9), custom_call_target="tpu_custom_call" | custom-call | tf_op jit(solution)/shard_map/pallas_call | solution.py:584
  176.5 1.3 copy.7

commit v3 on v2

--- a/solution.py
+++ b/solution.py
@@ -57,6 +57,7 @@
         self.leg_of = {"own": leg, "first": self.a1, "second": self.a2, "both": fx(fy(leg))}
         self.slot_of = {"own": 0, "first": self.first, "second": self.second, "both": 3}
         self.pending = []
+        self.partner_at = None
 
     def remote(self, src, dst, sem, index, to):
         return pltpu.make_async_remote_copy(
@@ -72,11 +73,6 @@
         copy.start()
         self.pending.append(copy)
 
-    def block(self, slot, h):
-        return self.ws.at[
-            slot, rows_at(self.own_at, self.own_rows), pl.ds(h * self.part, self.part), :
-        ]
-
     def piece(self, slot, h):
         return self.ws.at[
             slot, rows_at(self.left_at, self.n_left), pl.ds(h * self.part, self.part), :
@@ -93,8 +89,13 @@
         dst = {"a1": self.first, "own": self.second, "relay": 3}[kind]
         target = self.a1 if kind == "a1" else self.a2
         index = ({"a1": 0, "own": 1, "relay": 2}[kind], h)
-        source = self.block(dst if arriving else src, h)
-        return self.remote(source, self.block(dst, h), self.a_sem, index, self.to(target))
+        rows = rows_at(self.own_at, self.own_rows)
+        if kind != "a1" and self.partner_at is not None:
+            rows = rows_at(self.left_at if arriving else self.partner_at, self.n_left)
+        columns = pl.ds(h * self.part, self.part)
+        source = self.ws.at[dst if arriving else src, rows, columns, :]
+        place = self.ws.at[dst, rows, columns, :]
+        return self.remote(source, place, self.a_sem, index, self.to(target))
 
     def send_hop(self, kind, h):
         self.go(self.hop(kind, h, False))
@@ -164,7 +165,7 @@
     low_a, low_b1, low_bd, low_br, low_loc, low_share,
     mid_a, mid_b1, mid_bd, mid_br, mid_loc, mid_share,
     top_a, top_b1, top_bd, top_br, top_loc, top_share,
-    first_sem, mid_first, top_first, rs_sem, ag_sem, op_sem,
+    first_sem, mid_first, top_first, mixed_sem, rs_sem, ag_sem, op_sem,
     mate_sem, rs2_sem, ag2_sem, op2_sem, half_sem, quarter_sem, rs3_sem,
     wide, half_sum, half_in, side_sum, side_in, rows_out, rows_in,
 ):
@@ -186,12 +187,13 @@
     )
     mid = Level(
         env, ws_mid, wl_mid, (mid_a, mid_b1, mid_bd, mid_br, mid_loc, mid_share),
-        128, core * 128, near_x + 2 * near_y, near, far, 1,
+        128, core * 128, near_x + 2 * near_y, near, far, 2,
     )
     top = Level(
         env, ws_top, wl_top, (top_a, top_b1, top_bd, top_br, top_loc, top_share),
-        64, core * 128 + side * 64, far_x + 2 * far_y, far, near, 1,
-    )
+        64, core * 128 + side * 64, near_x + 2 * near_y, near, far, 1,
+    )
+    low.partner_at = 64 * pick(core, near_x + 2 - 2 * near_y, 1 - near_x + 2 * near_y)
     q = side * 2 + core
     mine, theirs = rows_at(core * 8, 8), rows_at(8 - core * 8, 8)
     mid_rows, mate_rows = rows_at(core * 128, 128), rows_at(128 - core * 128, 128)
@@ -214,17 +216,15 @@
 
     barrier = pltpu.get_barrier_semaphore()
 
-    @pl.loop(1, LEGS)
-    def _(d):
-        pl.semaphore_signal(barrier, inc=1, device_id=(leaf, (leg + d) % LEGS), device_id_type=MESH)
-
-    for peer in (mate, across, cross):
+    near_by = [(leaf, hop(leg)) for hop in (x_near, x_far, y_near, y_far)]
+    for peer in (*near_by, mate, across, cross):
         pl.semaphore_signal(barrier, inc=1, device_id=peer, device_id_type=MESH)
-    pl.semaphore_wait(barrier, LEGS + 2)
+    pl.semaphore_wait(barrier, len(near_by) + 3)
 
     for h in range(2):
         own_low[h].wait()
         low.send_hop("a1", h)
+        low.send_hop("own", h)
     mid_out = transfer(
         w_mid.at[mate_rows], ws_mid.at[0, mate_rows, mine, :], mid_first, (0,), mate
     )
@@ -242,9 +242,9 @@
     for h in range(2):
         low.spread("own", h)
 
-    def load_left(read, n_left, at):
+    def load_left(read, n_left, at, start=0):
         for t in range(2):
-            l_cat[t * n_left : (t + 1) * n_left] = read(t, rows_at(at, n_left))
+            l_cat[start + t * n_left : start + (t + 1) * n_left] = read(t, rows_at(at, n_left))
 
     def load_right(legs):
         for t in range(2):
@@ -258,7 +258,14 @@
         ys_0[span, :] = mixed[:, :128]
         ys_1[span, :] = mixed[:, 128:]
 
-    def mix_low(name):
+    def mixed_at(turn, arriving):
+        return by_row_mid.at[pl.ds(32 + turn * 16, 16), pl.ds(128 * arriving, 128), :]
+
+    def mixed_copy(turn, arriving):
+        source = mixed_at(turn, 1 if arriving else 0)
+        return transfer(source, mixed_at(turn, 1), mixed_sem, (turn,), (leaf, low.a2))
+
+    def mix_low(turn, name):
         slot = low.slot_of[name]
 
         @pl.loop(0, 16, unroll=2)
@@ -267,7 +274,22 @@
 
         @pl.loop(0, 16, unroll=4)
         def _(s):
-            mix_rows(slot, s, by_row_low[s], low.n_left)
+            mixed = jnp.dot(l_cat[...], by_row_low[s], preferred_element_type=F32)
+            span = pl.ds(slot * 16 + s, 128, stride=64)
+            ys_0[span, :] = mixed[:128, :128]
+            ys_1[span, :] = mixed[:128, 128:]
+            by_row_mid[32 + turn * 16 + s, :128, :] = mixed[128:].astype(BF)
+
+    def take_low(turn, name):
+        slot = low.slot_of[name]
+        mixed_copy(turn, True).wait_recv()
+
+        @pl.loop(0, 16, unroll=4)
+        def _(s):
+            mixed = by_row_mid[32 + turn * 16 + s, 128:, :].astype(F32)
+            span = pl.ds(slot * 16 + s, 128, stride=64)
+            ys_0[span, :] = mixed[:, :128]
+            ys_1[span, :] = mixed[:, 128:]
 
     def turn_mid(name, half):
         slot = mid.slot_of[name]
@@ -360,72 +382,79 @@
         ws_top[0, rows_at(top.own_at + n * 16, 16), :, :] = wide[:, :16, :].astype(BF)
 
     own_bank.wait()
-    load_left(lambda t, rows: bank[0, choice[t, 0], rows, :], low.n_left, low.left_at)
+    for start, at in ((0, low.left_at), (128, low.partner_at)):
+        load_left(lambda t, rows: bank[0, choice[t, 0], rows, :], 64, at, start)
     for t in range(2):
         right_t[t] = bank[1, choice[t, 1]].T
     load_right(low.slot_legs)
-    top.send_hop("a1", 0)
     own_mid.wait()
     transfer(
         w_mid.at[mid_rows], ws_mid.at[0, mid_rows, theirs, :], mid_first, (0,), mate
     ).wait_recv()
     mid_share("own")
     top.share("own", 0, top.own_at, 64, across)
-    mix_low("own")
-
+    mix_low(0, "own")
     for h in range(2):
-        low.recv_hop("a1", h)
-        low.send_hop("relay", h)
-        low.send_hop("own", h)
-        low.spread("first", h)
-        if h == 0:
-            for n in range(2):
-                low.relay("own", n)
+        low.recv_hop("own", h)
+        low.spread("second", h)
+    low.recv_hop("a1", 0)
+    low.send_hop("relay", 0)
+    mixed_copy(0, False).start()
+    low.spread("first", 0)
+    for h in range(2):
+        low.relay("own", h)
+    for h in range(2):
+        low.relay("second", h)
+    low.recv_hop("a1", 1)
+    low.send_hop("relay", 1)
+    low.spread("first", 1)
+    mix_low(1, "first")
+    mixed_copy(1, False).start()
+    low.recv_hop("relay", 0)
+    low.spread("both", 0)
     low.relay("first", 0)
-    mix_low("first")
+    low.recv_hop("relay", 1)
+    low.spread("both", 1)
+    for h in range(2):
+        mid.send_hop("a1", h)
+    low.relay("both", 0)
     low.relay("first", 1)
+    take_low(0, "second")
+    low.relay("both", 1)
+    take_low(1, "both")
+    for name in ("own", "first", "both", "second"):
+        for h in range(2):
+            low.arrive(name, h)
+    mid.recv_hop("a1", 0)
+    mid.send_hop("relay", 0)
+    mid.send_hop("own", 0)
+    for h in range(2):
+        mid.spread("own", h)
+    mid.spread("first", 0)
+    for turn in range(2):
+        mixed_copy(turn, False).wait_send()
+    low.finish_local()
+    contract(low)
+
+    sums[...] = acc[...].astype(BF)
+    ring_start(lambda one: sums.at[:, rows_at(one * 16, 16), :], lambda d: inbox.at[d], rs_sem)
+    mid.recv_hop("a1", 1)
+    mid.send_hop("relay", 1)
+    mid.send_hop("own", 1)
+    mid.spread("first", 1)
+    mid_share("first")
+    top.send_hop("a1", 0)
+    for h in range(2):
+        mid.relay("own", h)
+    mid.recv_hop("relay", 0)
+    mid.spread("both", 0)
     turn_mid("own", core)
     mid_shared("own")
     turn_mid("own", 1 - core)
-    mid.spread("own", 0)
-    for h in range(2):
-        low.recv_hop("relay", h)
-        low.spread("both", h)
-        low.recv_hop("own", h)
-        low.spread("second", h)
-        if h == 0:
-            low.relay("both", 0)
-            low.relay("second", 0)
-    mid.send_hop("a1", 0)
-    low.relay("both", 1)
-    mix_low("both")
-    low.relay("second", 1)
-    top.recv_hop("a1", 0)
-    top.send_hop("relay", 0)
-    top.send_hop("own", 0)
-    top.share("first", 0, top.own_at, 64, across)
-    mix_low("second")
-    mid.relay("own", 0)
-    mid.recv_hop("a1", 0)
-    mid.send_hop("relay", 0)
-    mid.send_hop("own", 0)
-    mid.spread("first", 0)
-    mid_share("first")
-    for name in ("own", "first", "both", "second"):
-        for h in range(2):
-            low.arrive(name, h)
-    low.finish_local()
-    contract(low)
-
-    sums[...] = acc[...].astype(BF)
-    ring_start(lambda one: sums.at[:, rows_at(one * 16, 16), :], lambda d: inbox.at[d], rs_sem)
+    mid.recv_hop("own", 0)
+    mid.spread("second", 0)
+    mid.relay("first", 0)
     turn_mid("first", core)
-    mid_shared("second")
-    turn_mid("second", 1 - core)
-    mid.recv_hop("relay", 0)
-    mid.spread("both", 0)
-    mid_share("both")
-    mid.relay("first", 0)
     ring_recv(lambda d: inbox.at[d], rs_sem)
     total = acc[:, rows_at(leg * 16, 16), :]
     for d in range(1, LEGS):
@@ -435,28 +464,38 @@
     ring_start(
         lambda one: block, lambda d: ops_a.at[core, :, rows_at(leg * 16, 16), :], ag_sem
     )
-    mid.recv_hop("own", 0)
-    mid.spread("second", 0)
+    top.recv_hop("a1", 0)
+    top.send_hop("relay", 0)
+    top.share("first", 0, top.own_at, 64, across)
+    mid.relay("first", 1)
+    mid_shared("second")
+    turn_mid("second", 1 - core)
+    mid.recv_hop("relay", 1)
+    mid.spread("both", 1)
+    mid_share("both")
+    mid.recv_hop("own", 1)
+    mid.spread("second", 1)
     mid_share("second")
+    top.send_hop("own", 0)
+    mid.relay("both", 0)
+    mid.relay("second", 0)
     turn_mid("both", core)
     turn_mid("second", core)
+    for name in ("both", "second"):
+        mid.relay(name, 1)
     ring_recv(
         lambda d: ops_a.at[core, :, rows_at((leg - d + LEGS) % LEGS * 16, 16), :], ag_sem
     )
     op_send = transfer(ops_a.at[core], ops_a.at[core], op_sem, (0,), mate)
     op_send.start()
-    mid.relay("both", 0)
     top.recv_hop("relay", 0)
     top.share("both", 0, top.own_at, 64, across)
-    top.recv_hop("own", 0)
-    top.share("second", 0, top.own_at, 64, across)
-    for name in ("own", "first", "both", "second"):
+    for name in ("own", "first"):
         top.spread(name, 0)
     mid_shared("both")
     turn_mid("both", 1 - core)
     mid_shared("first")
     turn_mid("first", 1 - core)
-    mid.relay("second", 0)
     low.finish()
     transfer(ops_a.at[1 - core], ops_a.at[1 - core], op_sem, (0,), mate).wait_recv()
 
@@ -465,8 +504,13 @@
         right_t[t] = ops_a[1, t].T
     load_right(mid.slot_legs)
     mix_mid()
+    top.recv_hop("own", 0)
+    top.share("second", 0, top.own_at, 64, across)
+    for name in ("both", "second"):
+        top.spread(name, 0)
     for name in ("own", "first", "both", "second"):
-        mid.arrive(name, 0)
+        for h in range(2):
+            mid.arrive(name, h)
     mid.finish_local()
     contract(mid)
 
@@ -600,7 +644,7 @@
             vmem((8192, 128), F32),
             vmem((2, 2, 256, BOND), BF),
             vmem((2, BOND, BOND), F32),
-            vmem((128, BOND), BF),
+            vmem((256, BOND), BF),
             vmem((128, BOND), BF),
             vmem((2, BOND, BOND), BF),
             vmem((2, 4, BOND, BOND), BF),
@@ -614,11 +658,12 @@
             vmem((16, BOND), BF),
             vmem((2, 2, BOND, BOND), BF),
             *level_sems(2),
-            *level_sems(1),
+            *level_sems(2),
             *level_sems(1),
             dma((5,)),
             dma((2, 1)),
             dma((2, 3)),
+            dma((2, 2)),
             dma((2, LEGS)),
             dma((2, LEGS)),
             dma((2, 1)),

time: 178 us -> 168 us (0.944)
  Pallas kernels: 177 us -> 166 us
    pallas_call x1, Pallas kernels: 177 us -> 166 us  [on_device(): pl.pallas_call(kernel, out_shape=jax.ShapeDtypeStruct((1, 2, 4, BOND), F3...]
where the time goes in v3:
time: 168 us
  Pallas kernels  166 us (99%)
    pallas_call x1, Pallas kernels, on_device(): pl.pallas_call(kernel, out_shape=jax.ShapeDtypeStruct((1, 2, 4, BOND), F3...  166 us

profile of v3, /device:TPU:1, one launch (start us, length us, event | category | flops | bytes accessed | tf_op | source)
XLA Modules:
  0.0 167.6 jit_solution(5775630011719461938)
XLA Ops:
  0.0 166.3 %shard_map.55 = f32[1,2,4,256]{3,2,1,0:T(4,128)} custom-call(bf16[256,16,256]{2,1,0:T(8,128)(2,1)} %bitcast.5, bf16[256,8,256]{2,1,0:T(8,128)(2,1)} %bitcast.6, bf16[256,4,256]{2,1,0:T(4,128)(2,1)} %bitcast.8, bf16[2,4,256,256]{3,2,1,0:T(8,128)(2,1)} %bitcast.7, s32[2,2]{1,0:T(2,128)} %bitcast.9), custom_call_target="tpu_custom_call" | custom-call | tf_op jit(solution)/shard_map/pallas_call | solution.py:628
  166.3 1.3 copy.7

commit v4 on v3

--- a/solution.py
+++ b/solution.py
@@ -304,20 +304,23 @@
         def _(s):
             mix_rows(0, s, by_row_mid[s], mid.n_left)
 
-    def turn_top(name):
+    def turn_top(name, half):
         slot = top.slot_of[name]
 
-        @pl.loop(0, 16, unroll=2)
+        @pl.loop(0, 8, unroll=2)
         def _(n):
-            turned = jnp.swapaxes(ws_top[slot, pl.ds(n * 16, 16)], 0, 1)
+            at = half * 8 + n
+            turned = jnp.swapaxes(ws_top[slot, rows_at(at * 16, 16)], 0, 1)
             for s in range(16):
-                ws_low[slot, s * 16 + n] = turned[s]
-
-    def mix_top():
-        @pl.loop(0, 64, unroll=8)
+                ws_low[slot, s * 16 + at] = turned[s]
+
+    def mix_top(name):
+        slot = top.slot_of[name]
+
+        @pl.loop(0, 16, unroll=8)
         def _(s):
-            rows = ws_low[s // 16, pl.ds(s % 16 * 16, 16)]
-            mix_rows(0, s, rows.reshape(256, BOND), top.n_left)
+            rows = ws_low[slot, pl.ds(s * 16, 16)]
+            mix_rows(slot, s, rows.reshape(256, BOND), top.n_left)
 
     def contract(level):
         acc[...] = jnp.zeros_like(acc)
@@ -362,6 +365,9 @@
 
     def mid_shared(name):
         mid.shared(name, 0, 128 - core * 128, 128, mate)
+
+    def top_shared(name):
+        top.shared(name, 1, 128 - core * 128, 128, mate)
 
     def top_across(name):
         top.shared(name, 0, core * 128 + (1 - side) * 64, 64, across)
@@ -431,6 +437,7 @@
     for h in range(2):
         mid.spread("own", h)
     mid.spread("first", 0)
+    top_across("own")
     for turn in range(2):
         mixed_copy(turn, False).wait_send()
     low.finish_local()
@@ -481,21 +488,17 @@
     mid.relay("second", 0)
     turn_mid("both", core)
     turn_mid("second", core)
-    for name in ("both", "second"):
-        mid.relay(name, 1)
+    mid.relay("both", 1)
     ring_recv(
         lambda d: ops_a.at[core, :, rows_at((leg - d + LEGS) % LEGS * 16, 16), :], ag_sem
     )
     op_send = transfer(ops_a.at[core], ops_a.at[core], op_sem, (0,), mate)
     op_send.start()
-    top.recv_hop("relay", 0)
-    top.share("both", 0, top.own_at, 64, across)
-    for name in ("own", "first"):
-        top.spread(name, 0)
     mid_shared("both")
     turn_mid("both", 1 - core)
     mid_shared("first")
     turn_mid("first", 1 - core)
+    top_across("first")
     low.finish()
     transfer(ops_a.at[1 - core], ops_a.at[1 - core], op_sem, (0,), mate).wait_recv()
 
@@ -504,10 +507,18 @@
         right_t[t] = ops_a[1, t].T
     load_right(mid.slot_legs)
     mix_mid()
+    mid.relay("second", 1)
+    top.recv_hop("relay", 0)
+    top.share("both", 0, top.own_at, 64, across)
+    for name in ("own", "first"):
+        top.spread(name, 0)
     top.recv_hop("own", 0)
     top.share("second", 0, top.own_at, 64, across)
     for name in ("both", "second"):
         top.spread(name, 0)
+    top_shared("own")
+    for half in range(2):
+        turn_top("own", half)
     for name in ("own", "first", "both", "second"):
         for h in range(2):
             mid.arrive(name, h)
@@ -518,23 +529,24 @@
     sums[...] = acc[...].astype(BF)
     mate_send = transfer(sums.at[1 - core], mate_in, mate_sem, (0,), mate)
     mate_send.start()
-    top_across("own")
-    top_across("first")
     transfer(mate_in, mate_in, mate_sem, (0,), mate).wait_recv()
     mid_sum[...] = (acc[core] + mate_in[...].astype(F32)).astype(BF)
     ring_start(lambda one: mid_sum.at[rows_at(one * 16, 16), :], lambda d: mid_in.at[d], rs2_sem)
     own_rows = rows_at(leg * 16, 16)
     total = acc[core, own_rows, :] + mate_in[own_rows, :].astype(F32)
-    top.shared("own", 1, 128 - core * 128, 128, mate)
-    turn_top("own")
-    top_across("both")
+    top_shared("second")
+    turn_top("second", 1 - core)
+    turn_top("first", core)
     ring_recv(lambda d: mid_in.at[d], rs2_sem)
     for d in range(1, LEGS):
         total = total + mid_in[d].astype(F32)
     mid_block[...] = total.astype(BF)
     ops_b[side, core, own_rows, :] = total.astype(BF)
     ring_start(lambda one: mid_block, lambda d: ops_b.at[side, core, own_rows, :], ag2_sem)
-    top_across("second")
+    top.relay("own", 0)
+    top.relay("first", 0)
+    top_across("both")
+    turn_top("both", core)
     ring_recv(
         lambda d: ops_b.at[side, core, rows_at((leg - d + LEGS) % LEGS * 16, 16), :], ag2_sem
     )
@@ -545,19 +557,16 @@
     ]
     for copy in op2_sends:
         copy.start()
-    top.shared("both", 1, 128 - core * 128, 128, mate)
-    turn_top("both")
-    top.relay("own", 0)
-    top.relay("first", 0)
+    top_shared("both")
+    turn_top("both", 1 - core)
+    top_across("second")
+    turn_top("second", core)
     top.relay("both", 0)
+    top.relay("second", 0)
     other = ops_b.at[1 - side, core]
     transfer(other, other, op2_sem, (1,), across).wait_recv()
     op2_sends.append(transfer(other, other, op2_sem, (2,), mate))
     op2_sends[-1].start()
-    top.relay("second", 0)
-    for name in ("first", "second"):
-        top.shared(name, 1, 128 - core * 128, 128, mate)
-        turn_top(name)
     for n, ref in ((0, ops_b.at[side, 1 - core]), (2, ops_b.at[1 - side, 1 - core])):
         transfer(ref, ref, op2_sem, (n,), mate).wait_recv()
 
@@ -565,7 +574,12 @@
     for t in range(2):
         right_t[t] = ops_b[1, t].T
     load_right(top.slot_legs)
-    mix_top()
+    mix_top("own")
+    mix_top("both")
+    top_shared("first")
+    turn_top("first", 1 - core)
+    mix_top("first")
+    mix_top("second")
     for name in ("own", "first", "both", "second"):
         top.arrive(name, 0)
     top.finish_local()

time: 168 us -> 167 us (level)
  no operation moved by 1% of the time
where the time goes in v4:
time: 167 us
  Pallas kernels  166 us (99%)
    pallas_call x1, Pallas kernels, on_device(): pl.pallas_call(kernel, out_shape=jax.ShapeDtypeStruct((1, 2, 4, BOND), F3...  166 us

profile of v4, /device:TPU:1, one launch (start us, length us, event | category | flops | bytes accessed | tf_op | source)
XLA Modules:
  0.0 166.9 jit_solution(3683682041910680421)
XLA Ops:
  0.0 165.6 %shard_map.55 = f32[1,2,4,256]{3,2,1,0:T(4,128)} custom-call(bf16[256,16,256]{2,1,0:T(8,128)(2,1)} %bitcast.5, bf16[256,8,256]{2,1,0:T(8,128)(2,1)} %bitcast.6, bf16[256,4,256]{2,1,0:T(4,128)(2,1)} %bitcast.8, bf16[2,4,256,256]{3,2,1,0:T(8,128)(2,1)} %bitcast.7, s32[2,2]{1,0:T(2,128)} %bitcast.9), custom_call_target="tpu_custom_call" | custom-call | tf_op jit(solution)/shard_map/pallas_call | solution.py:642
  165.6 1.3 copy.7

commit v5 on v4

--- a/solution.py
+++ b/solution.py
@@ -326,7 +326,7 @@
         acc[...] = jnp.zeros_like(acc)
         n_left = level.n_left
 
-        @pl.loop(0, n_left // 4, unroll=2)
+        @pl.loop(0, n_left // 4, unroll=4)
         def _(n):
             for k in range(4):
                 turned = jnp.dot(

time: 167 us -> 167 us (level)
  no operation moved by 1% of the time
where the time goes in v5:
time: 167 us
  Pallas kernels  165 us (99%)
    pallas_call x1, Pallas kernels, on_device(): pl.pallas_call(kernel, out_shape=jax.ShapeDtypeStruct((1, 2, 4, BOND), F3...  165 us

profile of v5, /device:TPU:1, one launch (start us, length us, event | category | flops | bytes accessed | tf_op | source)
XLA Modules:
  0.0 166.7 jit_solution(2742074339967900630)
XLA Ops:
  0.0 165.3 %shard_map.55 = f32[1,2,4,256]{3,2,1,0:T(4,128)} custom-call(bf16[256,16,256]{2,1,0:T(8,128)(2,1)} %bitcast.5, bf16[256,8,256]{2,1,0:T(8,128)(2,1)} %bitcast.6, bf16[256,4,256]{2,1,0:T(4,128)(2,1)} %bitcast.8, bf16[2,4,256,256]{3,2,1,0:T(8,128)(2,1)} %bitcast.7, s32[2,2]{1,0:T(2,128)} %bitcast.9), custom_call_target="tpu_custom_call" | custom-call | tf_op jit(solution)/shard_map/pallas_call | solution.py:642
  165.4 1.3 copy.7
